TPU v7x, 256 devices: a whole 4x4x8 slice. The times are simulated.
256 devices in a mesh: dp: 32 (over y, x, core), tensor: 8 (over z).
Axes of the slice: x: 4, y: 4, z: 8, core: 2. Of those that a mesh axis runs over, the one named last changes fastest.
Arguments:
- hidden: bfloat16 [32, 1024, 4096], P('dp', None, 'tensor'), as said below
- gain: float32 [4096], replicated, may hold values from 0.5 to 1.5
- head: bfloat16 [4096, 131072], P(None, ('dp', 'tensor'))
- lengths: int32 [32], P('dp'), may hold values from 256 to 1024, as said below
- offsets: int32 [32, 32], P('dp'), may hold values from 0 to 255
- targets: int32 [32, 32], P('dp'), may hold values from 0 to 131071
- mask: int32 [32, 32], P('dp'), may hold values from 0 to 1, as said below
Outputs:
- logprob: float32 [32, 32], P('dp')
- entropy: float32 [32, 32], P('dp')
Inputs may be any that keep to these rules, and one draw needn't show every extreme that they name: `lengths`: each length is at least 256; some sequence has length exactly 1024 in every draw. `mask`: among the 32 slots of the sequences of one index of dp, at most 16 are scored; some index of dp has exactly 16. `hidden`: entries are of order one or a few tens in magnitude.
All inputs are finite; a program needn't handle non-finite values.
Results may differ from a plain program's by a relative error of at most 0.0089.
Values may be sent and summed in bfloat16 or wider, within the bound.
A program may use at most 64 MiB of HBM per device.

v0:
```python
import jax
import jax.numpy as jnp
from jax import lax
from jax.sharding import PartitionSpec as P


def per_device(hidden, gain, head, lengths, offsets, targets, mask):
    seq_count, slot_count = offsets.shape
    local_rows = seq_count * slot_count
    position = lengths[:, None] - 1 - offsets
    picked = jnp.take_along_axis(hidden, position[:, :, None], axis=1)
    picked = picked.reshape(local_rows, hidden.shape[2])
    full_rows = lax.all_gather(picked, "tensor", axis=1, tiled=True)
    values = full_rows.astype(jnp.float32)
    meansq = jnp.mean(values * values, axis=-1, keepdims=True)
    normed = (values * lax.rsqrt(meansq + 1e-06) * gain).astype(jnp.bfloat16)
    flat_target = targets.reshape(local_rows)
    flat_mask = mask.reshape(local_rows)
    block_rows = normed.shape[0]
    vocab_width = head.shape[1]
    vocab_start = (
        lax.axis_index("dp") * lax.axis_size("tensor") + lax.axis_index("tensor")
    ) * vocab_width
    columns = jnp.arange(vocab_width, dtype=jnp.int32)
    rows_piece = lax.all_gather(normed, "dp", axis=0, tiled=True)
    target_piece = lax.all_gather(flat_target, "dp", axis=0, tiled=True)
    logits = jnp.dot(rows_piece, head, preferred_element_type=jnp.float32)
    top = jnp.max(logits, axis=-1)
    expo = jnp.exp(logits - top[:, None])
    total = jnp.sum(expo, axis=-1)
    weighted = jnp.sum(expo * logits, axis=-1)
    hit = columns[None, :] == (target_piece - vocab_start)[:, None]
    chosen = jnp.sum(jnp.where(hit, logits, 0.0), axis=-1)
    fresh = (top, total, weighted, chosen)
    stats = tuple((new for new in fresh))
    top = lax.pmax(stats[0], ("dp", "tensor"))
    factor = jnp.exp(stats[0] - top)
    total, weighted, chosen = lax.psum(
        (stats[1] * factor, stats[2] * factor, stats[3]), ("dp", "tensor")
    )
    lse = top + jnp.log(total)
    score = chosen - lse
    spread = lse - weighted / total
    offset_rows = lax.axis_index("dp") * block_rows
    score = lax.dynamic_slice_in_dim(score, offset_rows, block_rows)
    spread = lax.dynamic_slice_in_dim(spread, offset_rows, block_rows)
    keep = flat_mask.astype(jnp.float32)
    logprob = (keep * score).reshape(seq_count, slot_count)
    entropy = (keep * spread).reshape(seq_count, slot_count)
    return (logprob, entropy)


def solution(mesh):
    return jax.shard_map(
        per_device,
        mesh=mesh,
        in_specs=(
            P("dp", None, "tensor"),
            P(),
            P(None, ("dp", "tensor")),
            P("dp"),
            P("dp", None),
            P("dp", None),
            P("dp", None),
        ),
        out_specs=(P("dp", None), P("dp", None)),
        check_vma=False,
    )
```

profile of v0, /device:TPU:1, one launch (start us, length us, event | category | flops | bytes accessed | tf_op | source)
XLA Modules:
  0.0 265.7 jit_solution(5815184149624589043)
XLA Ops:
  7.2 0.0 copy-start
  7.2 0.0 all-gather.3.cloned.1.call-start
  7.9 0.7 fusion.7
  8.6 0.7 compare_and_fusion
  9.3 0.0 copy-done
  9.3 0.6 gather_fusion
  9.9 0.1 broadcast_select_fusion
  10.0 23.3 %all_gather.10 = bf16[32,4096]{1,0:T(8,128)(2,1)S(1)} all-gather(bf16[32,512]{1,0:T(8,128)(2,1)S(1)} %broadcast_select_fusion), channel_id=1, replica_groups=mesh['dp'=32,'tensor'=8] {'tensor'}, dimensions={1}, use_global_device_ids=true | all-gather | bytes 294912 | tf_op jit(solution)/shard_map/all_gather | solution.py:13
  33.3 0.2 fusion.1
  33.4 1.6 fusion.3
  35.0 0.0 all-gather.3.cloned.1.call-update
  35.0 1.3 dynamic-slice
  37.0 0.8 bitcast_dynamic-update-slice_fusion
  37.7 19.8 %all-reduce = s32[1024]{0:T(1024)S(1)} all-reduce(s32[1024]{0:T(1024)S(1)} %bitcast_dynamic-update-slice_fusion), channel_id=2, replica_groups=mesh['dp'=32,'tensor'=8] {'dp'}, use_global_device_ids=true, to_apply=%add | all-reduce | flops 1024 | bytes 8192
  57.6 41.2 %all-gather.3.cloned.1.call-done = bf16[1024,4096]{1,0:T(8,128)(2,1)} async-done(((bf16[32,4096]{1,0:T(8,128)(2,1)}), bf16[1024,4096]{1,0:T(8,128)(2,1)}) %all-gather.3.cloned.1.call-update) | async-done | bytes 8388624 | tf_op jit(solution)/shard_map/all_gather | solution.py:25
  98.8 8.3 %fusion.10 = (f32[1024]{0:T(1024)S(1)}, f32[1024,512]{0,1:T(8,128)S(1)}) fusion(bf16[1024,4096]{1,0:T(8,128)(2,1)} %all-gather.3.cloned.1.call-done, bf16[4096,512]{1,0:T(8,128)(2,1)} %param.9), kind=kOutput, calls=%fused_computation.30 | convolution fusion | flops 4295490560 | bytes 14684160 | tf_op jit(solution)/shard_map/dot_general | solution.py:27
  107.1 0.0 copy-start.1
  107.1 75.8 %pmax.7 = f32[1024]{0:T(1024)S(1)} all-reduce(f32[1024]{0:T(1024)S(1)} %get-tuple-element.14), channel_id=1, replica_groups=mesh['dp'=32,'tensor'=8] {'dp','tensor'}, use_global_device_ids=true, to_apply=%region_4.5 | all-reduce | flops 1024 | bytes 8192 | tf_op jit(solution)/shard_map/pmax | solution.py:36
  182.9 0.7 multiply_reduce_fusion
  183.6 74.6 %all-reduce.1 = (f32[1024]{0:T(1024)S(1)}, f32[1024]{0:T(1024)S(1)}, f32[1024]{0:T(1024)S(1)}) all-reduce(f32[1024]{0:T(1024)S(1)} %get-tuple-element.4, f32[1024]{0:T(1024)S(1)} %get-tuple-element.11, f32[1024]{0:T(1024)S(1)} %get-tuple-element.10), channel_id=1, replica_groups=mesh['dp'=32,'tensor'=8] {'dp','tensor'}, use_global_device_ids=true, to_apply=%region_2.3 | all-reduce | flops 3072 | bytes 24576 | tf_op jit(solution)/shard_map/psum | solution.py:38
  258.3 0.0 copy-done.1
  258.3 0.6 fusion.9
  (6 shorter events, 0.0 us)
Async XLA Ops:
  7.2 2.1 copy-start
  7.2 91.7 %all-gather.3.cloned.1.call-start = ((), (), s32[]{:S(2)}) async-start(), calls=%async_computation | async-start | bytes 8650752 | tf_op jit(solution)/shard_map/all_gather | solution.py:25
  107.1 151.1 %copy-start.1 = (s32[1,32]{1,0:T(1,128)S(1)}, s32[1,32]{1,0:T(1,128)}, u32[]{:S(2)}) copy-start(s32[1,32]{1,0:T(1,128)} %param.13) | copy-start | bytes 388
Sparse Core Ops, SparseCore 0:
  35.2 63.6 all-gather.2
where the time goes:
time: 266 us
  blocking collectives  194 us (73%)
  waiting for transfers between devices  41.3 us (16%)
  between operations  15.5 us (6%)
  matrix products  8.27 us (3%)
  other arithmetic  4.44 us (2%)
  local copies, waits for them, and re-layouts  2.68 us (1%)
    pmax x1, blocking collectives, per_device(): top = lax.pmax(stats[0], ('dp', 'tensor'))  75.8 us
    psum x1, blocking collectives, per_device(): lax.psum((stats[1] * factor, stats[2] * factor, stats[3]), ('dp', 'tensor'))  74.6 us
    all_gather x1, waiting for transfers between devices, per_device(): rows_piece = lax.all_gather(normed, 'dp', axis=0, tiled=True)  41.2 us
    all_gather x1, blocking collectives, per_device(): full_rows = lax.all_gather(picked, 'tensor', axis=1, tiled=True)  23.3 us
    unnamed x1, blocking collectives  19.8 us
    dot_general x1, matrix products, per_device(): logits = jnp.dot(rows_piece, head, preferred_element_type=jnp.float32)  8.27 us
  transfers between devices with their start and end apart: 1, of which 1 were waited for; matrix products, arithmetic and copies ran while one was open for 1% of the time, Pallas kernels for 0%

commit v1 on v0

v1 whole, which is shorter than its diff:
```python
import functools

import jax
import jax.numpy as jnp
from jax import lax
from jax.experimental import pallas as pl
from jax.experimental.pallas import tpu as pltpu
from jax.sharding import PartitionSpec as P

MESH = pl.DeviceIdType.MESH
LIVE = 16


def merge(parts):
    tops = parts[:, 0, :]
    top = jnp.max(tops, axis=0, keepdims=True)
    factor = jnp.exp(tops - top)
    total = jnp.sum(parts[:, 1, :] * factor, axis=0, keepdims=True)
    weighted = jnp.sum(parts[:, 2, :] * factor, axis=0, keepdims=True)
    chosen = jnp.sum(parts[:, 3, :], axis=0, keepdims=True)
    return jnp.concatenate([top, total, weighted, chosen], axis=0)


def stats_kernel(part_ref, out_ref, got1, sent, got2, send1, recv1, send2, recv2, local):
    n_dp = part_ref.shape[0]
    n_t = got2.shape[0]
    me = lax.axis_index("dp")
    mt = lax.axis_index("tensor")

    barrier = pltpu.get_barrier_semaphore()

    def greet_dp(i, carry):
        p = lax.rem(me + 1 + i, n_dp)
        pl.semaphore_signal(barrier, 1, device_id=(p, mt), device_id_type=MESH)
        return carry

    def greet_t(i, carry):
        q = lax.rem(mt + 1 + i, n_t)
        pl.semaphore_signal(barrier, 1, device_id=(me, q), device_id_type=MESH)
        return carry

    lax.fori_loop(0, n_dp - 1, greet_dp, 0)
    lax.fori_loop(0, n_t - 1, greet_t, 0)
    pl.semaphore_wait(barrier, n_dp - 1 + n_t - 1)

    def out1(p):
        return pltpu.make_async_remote_copy(
            src_ref=part_ref.at[p], dst_ref=got1.at[me], send_sem=send1.at[p],
            recv_sem=recv1.at[me], device_id=(p, mt), device_id_type=MESH)

    def in1(p):
        return pltpu.make_async_remote_copy(
            src_ref=part_ref.at[p], dst_ref=got1.at[p], send_sem=send1.at[p],
            recv_sem=recv1.at[p], device_id=(p, mt), device_id_type=MESH)

    def start1(i, carry):
        out1(lax.rem(me + 1 + i, n_dp)).start()
        return carry

    lax.fori_loop(0, n_dp - 1, start1, 0)
    own1 = pltpu.make_async_copy(part_ref.at[me], got1.at[me], local.at[0])
    own1.start()

    def finish1(i, carry):
        p = lax.rem(me + 1 + i, n_dp)
        in1(p).wait_recv()
        out1(p).wait_send()
        return carry

    lax.fori_loop(0, n_dp - 1, finish1, 0)
    own1.wait()

    sent[...] = merge(got1[...])

    def out2(q):
        return pltpu.make_async_remote_copy(
            src_ref=sent, dst_ref=got2.at[mt], send_sem=send2.at[q],
            recv_sem=recv2.at[mt], device_id=(me, q), device_id_type=MESH)

    def in2(q):
        return pltpu.make_async_remote_copy(
            src_ref=sent, dst_ref=got2.at[q], send_sem=send2.at[q],
            recv_sem=recv2.at[q], device_id=(me, q), device_id_type=MESH)

    def start2(i, carry):
        out2(lax.rem(mt + 1 + i, n_t)).start()
        return carry

    lax.fori_loop(0, n_t - 1, start2, 0)
    own2 = pltpu.make_async_copy(sent, got2.at[mt], local.at[1])
    own2.start()

    def finish2(i, carry):
        q = lax.rem(mt + 1 + i, n_t)
        in2(q).wait_recv()
        out2(q).wait_send()
        return carry

    lax.fori_loop(0, n_t - 1, finish2, 0)
    own2.wait()

    out_ref[...] = merge(got2[...])


def exchange_stats(parts, n_t):
    n_dp, four, k = parts.shape
    return pl.pallas_call(
        stats_kernel,
        out_shape=jax.ShapeDtypeStruct((four, k), jnp.float32),
        in_specs=[pl.BlockSpec(memory_space=pltpu.VMEM)],
        out_specs=pl.BlockSpec(memory_space=pltpu.VMEM),
        scratch_shapes=[
            pltpu.VMEM((n_dp, four, k), jnp.float32),
            pltpu.VMEM((four, k), jnp.float32),
            pltpu.VMEM((n_t, four, k), jnp.float32),
            pltpu.SemaphoreType.DMA((n_dp,)),
            pltpu.SemaphoreType.DMA((n_dp,)),
            pltpu.SemaphoreType.DMA((n_t,)),
            pltpu.SemaphoreType.DMA((n_t,)),
            pltpu.SemaphoreType.DMA((2,)),
        ],
        compiler_params=pltpu.CompilerParams(collective_id=0, has_side_effects=True),
    )(parts)


def per_device(hidden, gain, head, lengths, offsets, targets, mask):
    seq_count, slot_count = offsets.shape
    slots = seq_count * slot_count
    maxlen = hidden.shape[1]
    n_dp = lax.axis_size("dp")
    n_t = lax.axis_size("tensor")
    k = min(LIVE, slots)

    live = mask.reshape(slots) != 0
    rank = jnp.cumsum(live.astype(jnp.int32)) - 1
    sel = live[None, :] & (rank[None, :] == jnp.arange(k, dtype=jnp.int32)[:, None])
    idx = jnp.sum(jnp.where(sel, jnp.arange(slots, dtype=jnp.int32)[None, :], 0), axis=1)
    seq_of = idx // slot_count
    position = lengths[seq_of] - 1 - offsets.reshape(slots)[idx]
    flat_hidden = hidden.reshape(seq_count * maxlen, hidden.shape[2])
    picked = jnp.take(flat_hidden, seq_of * maxlen + position, axis=0)
    flat_target = targets.reshape(slots)[idx]

    full_rows = lax.all_gather(picked, "tensor", axis=1, tiled=True)
    values = full_rows.astype(jnp.float32)
    meansq = jnp.mean(values * values, axis=-1, keepdims=True)
    normed = (values * lax.rsqrt(meansq + 1e-06) * gain).astype(jnp.bfloat16)

    vocab_width = head.shape[1]
    vocab_start = (lax.axis_index("dp") * n_t + lax.axis_index("tensor")) * vocab_width
    columns = jnp.arange(vocab_width, dtype=jnp.int32)
    rows_piece = lax.all_gather(normed, "dp", axis=0, tiled=True)
    target_piece = lax.all_gather(flat_target, "dp", axis=0, tiled=True)
    logits = jnp.dot(rows_piece, head, preferred_element_type=jnp.float32)
    top = jnp.max(logits, axis=-1)
    expo = jnp.exp(logits - top[:, None])
    total = jnp.sum(expo, axis=-1)
    weighted = jnp.sum(expo * logits, axis=-1)
    hit = columns[None, :] == (target_piece - vocab_start)[:, None]
    chosen = jnp.sum(jnp.where(hit, logits, 0.0), axis=-1)

    parts = jnp.stack([top, total, weighted, chosen]).reshape(4, n_dp, k).transpose(1, 0, 2)
    top, total, weighted, chosen = exchange_stats(parts, n_t)
    lse = top + jnp.log(total)
    score = chosen - lse
    spread = lse - weighted / total

    logprob = jnp.sum(jnp.where(sel, score[:, None], 0.0), axis=0)
    entropy = jnp.sum(jnp.where(sel, spread[:, None], 0.0), axis=0)
    return (logprob.reshape(seq_count, slot_count), entropy.reshape(seq_count, slot_count))


def solution(mesh):
    return jax.shard_map(
        per_device,
        mesh=mesh,
        in_specs=(
            P("dp", None, "tensor"),
            P(),
            P(None, ("dp", "tensor")),
            P("dp"),
            P("dp", None),
            P("dp", None),
            P("dp", None),
        ),
        out_specs=(P("dp", None), P("dp", None)),
        check_vma=False,
    )
```

time: 266 us -> 125 us (0.47)
  blocking collectives: 194 us -> 42.7 us
  Pallas kernels: 0 us -> 16.8 us
  waiting for transfers between devices: 41.3 us -> 33.8 us
    pmax x1 -> x0, blocking collectives: 75.8 us -> none  [per_device(): top = lax.pmax(stats[0], ('dp', 'tensor'))]
    psum x1 -> x0, blocking collectives: 74.6 us -> none  [per_device(): lax.psum((stats[1] * factor, stats[2] * factor, stats[3]), ('dp', 'tensor'))]
    pallas_call x0 -> x1, Pallas kernels: none -> 16.8 us  [exchange_stats(): pl.pallas_call(stats_kernel, out_shape=jax.ShapeDtypeStruct((four, k), jn...]
    all_gather x1, waiting for transfers between devices: 41.2 us -> 33.8 us  [per_device(): rows_piece = lax.all_gather(normed, 'dp', axis=0, tiled=True)]
  transfers between devices with their start and end apart: 1 -> 1, of which waited for: 1 -> 1; matrix products, arithmetic and copies ran while one was open for 1% -> 2% of each run, Pallas kernels for 0% -> 0%
where the time goes in v1:
time: 125 us
  blocking collectives  42.7 us (34%)
  waiting for transfers between devices  33.8 us (27%)
  Pallas kernels  16.8 us (13%)
  between operations  15.5 us (12%)
  matrix products  5.85 us (5%)
  other arithmetic  5.18 us (4%)
  local copies, waits for them, and re-layouts  5.14 us (4%)
    all_gather x1, waiting for transfers between devices, per_device(): rows_piece = lax.all_gather(normed, 'dp', axis=0, tiled=True)  33.8 us
    all_gather x1, blocking collectives, per_device(): full_rows = lax.all_gather(picked, 'tensor', axis=1, tiled=True)  23 us
    unnamed x1, blocking collectives  19.7 us
    pallas_call x1, Pallas kernels, exchange_stats(): pl.pallas_call(stats_kernel, out_shape=jax.ShapeDtypeStruct((four, k), jn...  16.8 us
    dot_general x1, matrix products, per_device(): logits = jnp.dot(rows_piece, head, preferred_element_type=jnp.float32)  5.85 us
  transfers between devices with their start and end apart: 1, of which 1 were waited for; matrix products, arithmetic and copies ran while one was open for 2% of the time, Pallas kernels for 0%

profile of v1, /device:TPU:1, one launch (start us, length us, event | category | flops | bytes accessed | tf_op | source)
XLA Modules:
  0.0 125.0 jit_solution(8410473039691137506)
XLA Ops:
  7.2 0.0 copy-start
  7.2 0.0 all-gather.3.cloned.1.call-start
  8.0 0.7 compare_bitcast_fusion
  8.6 0.1 copy.15
  8.7 0.1 reduce-window.8
  8.8 0.1 add_reduce_fusion
  8.9 0.1 select_reduce_fusion.3
  9.0 1.3 %gather_fusion = s32[16]{0:T(128)S(1)} fusion(s32[32]{0:T(128)} %bitcast.43, s32[1024]{0:T(1024)S(1)} %pad_clamp_fusion.1), kind=kCustom, calls=%fused_computation | custom fusion | bytes 192 | tf_op jit(solution)/shard_map/gather | solution.py:139
  10.4 0.0 copy-done
  10.4 0.6 gather_fusion.1
  11.0 0.1 broadcast_select_fusion
  11.1 23.0 %all_gather.9 = bf16[16,4096]{1,0:T(8,128)(2,1)S(1)} all-gather(bf16[16,512]{1,0:T(8,128)(2,1)S(1)} %broadcast_select_fusion), channel_id=1, replica_groups=mesh['dp'=32,'tensor'=8] {'tensor'}, dimensions={1}, use_global_device_ids=true | all-gather | bytes 147456 | tf_op jit(solution)/shard_map/all_gather | solution.py:144
  34.1 0.1 fusion.1
  34.3 1.5 %fusion.3 = bf16[16,4096]{1,0:T(8,128)(2,1)} fusion(bf16[16,4096]{1,0:T(8,128)(2,1)S(1)} %all_gather.9, f32[4096]{0:T(1024)} %param.8, f32[16]{0:T(128)S(1)} %add_rsqrt_fusion), kind=kLoop, calls=%fused_computation.12 | loop fusion | flops 262144 | bytes 278592 | tf_op jit(solution)/shard_map/convert_element_type | solution.py:147
  35.7 0.0 all-gather.3.cloned.1.call-update
  35.7 1.3 %gather_fusion.2 = s32[16]{0:T(128)S(1)} fusion(s32[32]{0:T(128)} %bitcast.44, s32[1024]{0:T(1024)S(1)} %pad_clamp_fusion.1), kind=kCustom, calls=%fused_computation.2 | custom fusion | bytes 192 | tf_op jit(solution)/shard_map/gather | solution.py:142
  37.1 1.3 %dynamic-slice = u32[1]{0:T(128)} dynamic-slice(u32[256]{0:T(256)} %constant.75, u32[]{:T(128)S(6)} %add.94), dynamic_slice_sizes={1} | dynamic-slice | bytes 12
  39.0 0.2 dynamic-update-slice
  39.2 19.7 %all-reduce = s32[512]{0:T(512)S(1)} all-reduce(s32[512]{0:T(512)S(1)} %dynamic-update-slice), channel_id=2, replica_groups=mesh['dp'=32,'tensor'=8] {'dp'}, use_global_device_ids=true, to_apply=%add | all-reduce | flops 512 | bytes 4096
  58.9 33.8 %all-gather.3.cloned.1.call-done = bf16[512,4096]{1,0:T(8,128)(2,1)} async-done(((bf16[16,4096]{1,0:T(8,128)(2,1)}), bf16[512,4096]{1,0:T(8,128)(2,1)}) %all-gather.3.cloned.1.call-update) | async-done | bytes 4194320 | tf_op jit(solution)/shard_map/all_gather | solution.py:152
  92.7 5.9 %fusion.8 = (f32[512]{0:T(512)S(1)}, f32[512,512]{0,1:T(8,128)S(1)}) fusion(bf16[512,4096]{1,0:T(8,128)(2,1)} %all-gather.3.cloned.1.call-done, bf16[4096,512]{1,0:T(8,128)(2,1)} %param.9), kind=kOutput, calls=%fused_computation.47 | convolution fusion | flops 2147745280 | bytes 9439232 | tf_op jit(solution)/shard_map/dot_general | solution.py:154
  98.6 0.1 stack.15
  98.7 0.3 fusion
  99.0 0.1 stack.16
  99.1 0.1 stack.17
  99.2 0.1 stack.18
  99.3 0.7 maximum_bitcast_fusion.part_ref
  100.0 16.8 %shard_map.86 = f32[4,16]{1,0:T(4,128)} custom-call(f32[32,4,16]{2,1,0:T(4,128)} %maximum_bitcast_fusion.part_ref), custom_call_target="tpu_custom_call" | custom-call | tf_op jit(solution)/shard_map/pallas_call | solution.py:107
  116.8 0.8 subtract_bitcast_fusion.1
  117.6 0.6 select_reduce_fusion.1
  (8 shorter events, 0.1 us)
Async XLA Ops:
  7.2 3.2 %copy-start = (bf16[1,1024,512]{2,1,0:T(8,128)(2,1)S(1)}, bf16[1,1024,512]{2,1,0:T(8,128)(2,1)}, u32[]{:S(2)}) copy-start(bf16[1,1024,512]{2,1,0:T(8,128)(2,1)} %param.7) | copy-start | bytes 3145732
  7.2 85.6 %all-gather.3.cloned.1.call-start = ((), (), s32[]{:S(2)}) async-start(), calls=%async_computation | async-start | bytes 4325376 | tf_op jit(solution)/shard_map/all_gather | solution.py:152
Sparse Core Ops, SparseCore 0:
  35.9 56.8 all-gather.2

commit v2 on v1

--- a/solution.py
+++ b/solution.py
@@ -149,8 +149,14 @@
     vocab_width = head.shape[1]
     vocab_start = (lax.axis_index("dp") * n_t + lax.axis_index("tensor")) * vocab_width
     columns = jnp.arange(vocab_width, dtype=jnp.int32)
-    rows_piece = lax.all_gather(normed, "dp", axis=0, tiled=True)
-    target_piece = lax.all_gather(flat_target, "dp", axis=0, tiled=True)
+    width = normed.shape[1]
+    digits = jnp.stack([flat_target // 65536, (flat_target // 256) % 256, flat_target % 256], axis=1)
+    tail = jnp.zeros((k, 128), jnp.bfloat16).at[:, :3].set(digits.astype(jnp.bfloat16))
+    block = jnp.concatenate([normed, tail], axis=1)
+    gathered = lax.all_gather(block, "dp", axis=0, tiled=True)
+    rows_piece = gathered[:, :width]
+    got_digits = gathered[:, width : width + 3].astype(jnp.int32)
+    target_piece = got_digits[:, 0] * 65536 + got_digits[:, 1] * 256 + got_digits[:, 2]
     logits = jnp.dot(rows_piece, head, preferred_element_type=jnp.float32)
     top = jnp.max(logits, axis=-1)
     expo = jnp.exp(logits - top[:, None])

time: 125 us -> 130 us (1.040)
  waiting for transfers between devices: 33.8 us -> 57.2 us
  blocking collectives: 42.7 us -> 23 us
  other arithmetic: 5.18 us -> 7.83 us
  local copies, waits for them, and re-layouts: 5.14 us -> 3.73 us
    all_gather x1, waiting for transfers between devices: 33.8 us -> 57.2 us  [per_device(): gathered = lax.all_gather(block, 'dp', axis=0, tiled=True)]
    unnamed x1 -> x0, blocking collectives: 19.7 us -> none
    unnamed x5 -> x2, local copies, waits for them, and re-layouts: 1.52 us -> 0.01 us
    another operation x1 -> x5, other arithmetic: 0.06 us -> 1.38 us
  transfers between devices with their start and end apart: 1 -> 1, of which waited for: 1 -> 1; matrix products, arithmetic and copies ran while one was open for 2% -> 0% of each run, Pallas kernels for 0% -> 0%
where the time goes in v2:
time: 130 us; the launch traced here: 129 us
  waiting for transfers between devices  57.2 us (44%)
  blocking collectives  23 us (18%)
  Pallas kernels  16.8 us (13%)
  between operations  14.8 us (11%)
  other arithmetic  7.83 us (6%)
  matrix products  5.85 us (4%)
  local copies, waits for them, and re-layouts  3.73 us (3%)
    all_gather x1, waiting for transfers between devices, per_device(): gathered = lax.all_gather(block, 'dp', axis=0, tiled=True)  57.2 us
    all_gather x1, blocking collectives, per_device(): full_rows = lax.all_gather(picked, 'tensor', axis=1, tiled=True)  23 us
    pallas_call x1, Pallas kernels, exchange_stats(): pl.pallas_call(stats_kernel, out_shape=jax.ShapeDtypeStruct((four, k), jn...  16.8 us
    dot_general x1, matrix products, per_device(): logits = jnp.dot(rows_piece, head, preferred_element_type=jnp.float32)  5.85 us
  transfers between devices with their start and end apart: 1, of which 1 were waited for; matrix products, arithmetic and copies ran while one was open for 0% of the time, Pallas kernels for 0%

profile of v2, /device:TPU:1, one launch (start us, length us, event | category | flops | bytes accessed | tf_op | source)
XLA Modules:
  0.0 129.3 jit_solution(9753916156582234768)
XLA Ops:
  7.2 0.0 copy-start
  7.2 0.0 all-gather.2.cloned.1.call-start
  7.2 0.7 compare_bitcast_fusion
  8.0 0.1 copy.43
  8.1 0.1 reduce-window.8
  8.1 0.1 add_reduce_fusion
  8.2 0.1 select_reduce_fusion.3
  9.0 1.3 %gather_fusion = s32[16]{0:T(128)S(1)} fusion(s32[32]{0:T(128)} %bitcast.61, s32[1024]{0:T(1024)S(1)} %pad_clamp_fusion.1), kind=kCustom, calls=%fused_computation | custom fusion | bytes 192 | tf_op jit(solution)/shard_map/gather | solution.py:139
  10.4 0.6 compare_reduce_fusion
  11.0 0.0 copy-done
  11.0 0.6 gather_fusion.1
  11.6 0.1 broadcast_select_fusion
  11.7 23.0 %all_gather.6 = bf16[16,4096]{1,0:T(8,128)(2,1)S(1)} all-gather(bf16[16,512]{1,0:T(8,128)(2,1)S(1)} %broadcast_select_fusion), channel_id=1, replica_groups=mesh['dp'=32,'tensor'=8] {'tensor'}, dimensions={1}, use_global_device_ids=true | all-gather | bytes 147456 | tf_op jit(solution)/shard_map/all_gather | solution.py:144
  34.7 0.1 fusion.4
  34.9 1.3 %gather_fusion.2 = s32[16]{0:T(128)S(1)} fusion(s32[32]{0:T(128)} %bitcast.62, s32[1024]{0:T(1024)S(1)} %pad_clamp_fusion.1), kind=kCustom, calls=%fused_computation.2 | custom fusion | bytes 192 | tf_op jit(solution)/shard_map/gather | solution.py:142
  36.3 0.1 copy.44
  36.3 0.8 fusion.6
  37.2 0.7 broadcast_select_fusion.1
  37.8 0.7 fusion.10
  38.5 0.0 all-gather.2.cloned.1.call-update
  38.5 57.2 %all-gather.2.cloned.1.call-done = bf16[512,4224]{1,0:T(8,128)(2,1)} async-done(((bf16[16,4224]{1,0:T(8,128)(2,1)}), bf16[512,4224]{1,0:T(8,128)(2,1)}) %all-gather.2.cloned.1.call-update) | async-done | bytes 4325392 | tf_op jit(solution)/shard_map/all_gather | solution.py:156
  95.7 5.8 %fusion.19 = (f32[512]{0:T(512)S(1)}, f32[512,512]{0,1:T(8,128)S(1)}) fusion(bf16[4096,512]{1,0:T(8,128)(2,1)} %param.11, bf16[512,4224]{1,0:T(8,128)(2,1)} %all-gather.2.cloned.1.call-done), kind=kOutput, calls=%fused_computation.78 | convolution fusion | flops 2147745280 | bytes 9439232 | tf_op jit(solution)/shard_map/dot_general | solution.py:160
  101.6 0.1 stack.23
  101.7 0.9 slice_convert_fusion
  102.6 0.3 fusion.8
  102.9 0.3 fusion.2
  103.3 0.1 stack.24
  103.3 0.1 stack.25
  103.4 0.1 stack.26
  103.5 0.7 maximum_bitcast_fusion.part_ref
  104.2 16.8 %shard_map.86 = f32[4,16]{1,0:T(4,128)} custom-call(f32[32,4,16]{2,1,0:T(4,128)} %maximum_bitcast_fusion.part_ref), custom_call_target="tpu_custom_call" | custom-call | tf_op jit(solution)/shard_map/pallas_call | solution.py:107
  121.0 0.8 subtract_bitcast_fusion.1
  121.8 0.6 select_reduce_fusion.1
  (8 shorter events, 0.1 us)
Async XLA Ops:
  7.2 3.9 %copy-start = (bf16[1,1024,512]{2,1,0:T(8,128)(2,1)S(1)}, bf16[1,1024,512]{2,1,0:T(8,128)(2,1)}, u32[]{:S(2)}) copy-start(bf16[1,1024,512]{2,1,0:T(8,128)(2,1)} %param.9) | copy-start | bytes 3145732
  7.2 88.6 %all-gather.2.cloned.1.call-start = ((), (), s32[]{:S(2)}) async-start(), calls=%async_computation | async-start | bytes 4460544 | tf_op jit(solution)/shard_map/all_gather | solution.py:156
Sparse Core Ops, SparseCore 0:
  38.6 57.0 all-gather.1

commit v3 on v1

--- a/solution.py
+++ b/solution.py
@@ -141,15 +141,16 @@
     picked = jnp.take(flat_hidden, seq_of * maxlen + position, axis=0)
     flat_target = targets.reshape(slots)[idx]
 
-    full_rows = lax.all_gather(picked, "tensor", axis=1, tiled=True)
-    values = full_rows.astype(jnp.float32)
-    meansq = jnp.mean(values * values, axis=-1, keepdims=True)
-    normed = (values * lax.rsqrt(meansq + 1e-06) * gain).astype(jnp.bfloat16)
+    width = picked.shape[1]
+    raw = lax.all_gather(picked, ("dp", "tensor"), axis=0, tiled=True).reshape(n_dp, n_t, k, width)
+    values = raw.astype(jnp.float32)
+    meansq = jnp.sum(values * values, axis=(1, 3), keepdims=True) / (n_t * width)
+    scaled = values * lax.rsqrt(meansq + 1e-06) * gain.reshape(1, n_t, 1, width)
+    rows_piece = scaled.astype(jnp.bfloat16).transpose(0, 2, 1, 3).reshape(n_dp * k, n_t * width)
 
     vocab_width = head.shape[1]
     vocab_start = (lax.axis_index("dp") * n_t + lax.axis_index("tensor")) * vocab_width
     columns = jnp.arange(vocab_width, dtype=jnp.int32)
-    rows_piece = lax.all_gather(normed, "dp", axis=0, tiled=True)
     target_piece = lax.all_gather(flat_target, "dp", axis=0, tiled=True)
     logits = jnp.dot(rows_piece, head, preferred_element_type=jnp.float32)
     top = jnp.max(logits, axis=-1)

time: 125 us -> 172 us (1.38)
  waiting for transfers between devices: 33.8 us -> 101 us
  blocking collectives: 42.7 us -> 14.4 us
  other arithmetic: 5.18 us -> 15.4 us
  matrix products: 5.85 us -> 2.39 us
  local copies, waits for them, and re-layouts: 5.14 us -> 8.26 us
  Pallas kernels: 16.8 us -> 14.9 us
    all_gather x1, waiting for transfers between devices: 33.8 us -> 101 us  [per_device(): lax.all_gather(picked, ('dp', 'tensor'), axis=0, tiled=True)]
    all_gather x1 -> x0, blocking collectives: 23 us -> none  [per_device(): full_rows = lax.all_gather(picked, 'tensor', axis=1, tiled=True)]
    convert_element_type x1 -> x2, other arithmetic: 1.46 us -> 8.15 us  [the longest x1 4.83 us: per_device(): scaled.astype(jnp.bfloat16).transpose(0, 2, 1, 3)]
    unnamed x1, blocking collectives: 19.7 us -> 14.4 us
    dot_general x1, matrix products: 5.85 us -> 2.39 us  [per_device(): logits = jnp.dot(rows_piece, head, preferred_element_type=jnp.float32)]
    reduce_sum x1 -> x2, other arithmetic: 0.15 us -> 3.12 us  [per_device(): jnp.sum(values * values, axis=(1, 3), keepdims=True) / (n_t * width)]
    unnamed x5 -> x8, local copies, waits for them, and re-layouts: 1.52 us -> 3.82 us
    pallas_call x1, Pallas kernels: 16.8 us -> 14.9 us  [exchange_stats(): pl.pallas_call(stats_kernel, out_shape=jax.ShapeDtypeStruct((four, k), jn...]
where the time goes in v3:
time: 172 us
  waiting for transfers between devices  101 us (59%)
  between operations  15.6 us (9%)
  other arithmetic  15.4 us (9%)
  Pallas kernels  14.9 us (9%)
  blocking collectives  14.4 us (8%)
  local copies, waits for them, and re-layouts  8.26 us (5%)
  matrix products  2.39 us (1%)
    all_gather x1, waiting for transfers between devices, per_device(): lax.all_gather(picked, ('dp', 'tensor'), axis=0, tiled=True)  101 us
    pallas_call x1, Pallas kernels, exchange_stats(): pl.pallas_call(stats_kernel, out_shape=jax.ShapeDtypeStruct((four, k), jn...  14.9 us
    unnamed x1, blocking collectives  14.4 us
    convert_element_type x1, other arithmetic, per_device(): scaled.astype(jnp.bfloat16).transpose(0, 2, 1, 3)  4.83 us
    unnamed x8, local copies, waits for them, and re-layouts  3.82 us
  transfers between devices with their start and end apart: 1, of which 1 were waited for; matrix products, arithmetic and copies ran while one was open for 2% of the time, Pallas kernels for 0%

profile of v3, /device:TPU:1, one launch (start us, length us, event | category | flops | bytes accessed | tf_op | source)
XLA Modules:
  0.0 171.9 jit_solution(5540435085048655388)
XLA Ops:
  7.2 0.0 copy-start
  7.2 0.0 all-gather.3.cloned.1.call-start
  8.0 0.7 compare_bitcast_fusion
  8.6 0.1 copy.16
  8.7 0.1 reduce-window.8
  8.8 0.1 add_reduce_fusion
  8.9 0.1 select_reduce_fusion.3
  9.0 1.3 gather_fusion
  10.4 0.0 copy-done
  10.4 0.6 gather_fusion.1
  11.0 0.7 broadcast_select_fusion
  11.7 0.0 all-gather.3.cloned.1.call-update
  11.7 1.3 gather_fusion.2
  13.0 0.7 mul.50
  13.7 1.3 dynamic-slice
  15.7 0.2 dynamic-update-slice
  15.9 14.4 %all-reduce = s32[512]{0:T(512)S(1)} all-reduce(s32[512]{0:T(512)S(1)} %dynamic-update-slice), channel_id=2, replica_groups=mesh['dp'=32,'tensor'=8] {'dp'}, use_global_device_ids=true, to_apply=%add | all-reduce | flops 512 | bytes 4096
  30.4 100.8 %all-gather.3.cloned.1.call-done = bf16[4096,512]{1,0:T(8,128)(2,1)} async-done(((bf16[16,512]{1,0:T(8,128)(2,1)}), bf16[4096,512]{1,0:T(8,128)(2,1)}) %all-gather.3.cloned.1.call-update) | async-done | bytes 4194320 | tf_op jit(solution)/shard_map/all_gather | solution.py:145
  131.2 3.1 %multiply_reduce_fusion = f32[4096]{0:T(1024)S(1)} fusion(bf16[4096,512]{1,0:T(8,128)(2,1)} %all-gather.3.cloned.1.call-done), kind=kLoop, calls=%fused_computation.6 | loop fusion | flops 6287360 | bytes 4210688 | tf_op jit(solution)/shard_map/reduce_sum | solution.py:147
  134.3 0.1 reduce_sum.75
  134.4 3.3 %convert.12 = f32[32,8,16,512]{3,2,1,0:T(8,128)S(1)} convert(bf16[32,8,16,512]{3,2,1,0:T(8,128)(2,1)} %bitcast.51) | non-fusion elementwise | flops 2097152 | bytes 12582912 | tf_op jit(solution)/shard_map/convert_element_type | solution.py:146
  137.8 4.8 %fusion.1 = bf16[32,8,16,512]{3,1,2,0:T(8,128)(2,1)S(1)} fusion(f32[32,8,16,512]{3,2,1,0:T(8,128)S(1)} %convert.12, f32[8,512]{1,0:T(8,128)S(1)} %mul.50, f32[32,16]{1,0:T(8,128)S(1)} %add_rsqrt_fusion), kind=kLoop, calls=%fused_computation.5 | loop fusion | flops 6291456 | bytes 12601344 | tf_op jit(solution)/shard_map/convert_element_type | solution.py:149
  142.6 0.0 copy-start.1
  142.6 2.3 %copy.22 = bf16[64,8,8,512]{3,1,2,0:T(8,128)(2,1)S(1)} copy(bf16[64,8,8,512]{3,2,1,0:T(8,128)(2,1)S(1)} %bitcast.52) | data formatting | bytes 8388608
  144.9 0.0 copy-done.1
  144.9 2.4 %fusion.7 = (f32[512]{0:T(512)S(1)}, f32[512,512]{0,1:T(8,128)S(1)}) fusion(bf16[512,4096]{1,0:T(8,128)(2,1)S(1)} %bitcast.53, bf16[4096,512]{1,0:T(8,128)(2,1)S(1)} %copy-done.1), kind=kOutput, calls=%fused_computation.46 | convolution fusion | flops 2147745280 | bytes 9439232 | tf_op jit(solution)/shard_map/dot_general | solution.py:155
  147.3 0.1 stack.15
  147.4 0.3 fusion.2
  147.8 0.1 stack.16
  147.8 0.1 stack.17
  147.9 0.1 stack.18
  148.0 0.7 maximum_bitcast_fusion.part_ref
  148.7 14.9 %shard_map.86 = f32[4,16]{1,0:T(4,128)} custom-call(f32[32,4,16]{2,1,0:T(4,128)} %maximum_bitcast_fusion.part_ref), custom_call_target="tpu_custom_call" | custom-call | tf_op jit(solution)/shard_map/pallas_call | solution.py:107
  163.6 0.8 subtract_bitcast_fusion.1
  164.4 0.6 select_reduce_fusion.1
  (9 shorter events, 0.1 us)
Async XLA Ops:
  7.2 3.2 %copy-start = (bf16[1,1024,512]{2,1,0:T(8,128)(2,1)S(1)}, bf16[1,1024,512]{2,1,0:T(8,128)(2,1)}, u32[]{:S(2)}) copy-start(bf16[1,1024,512]{2,1,0:T(8,128)(2,1)} %param.7) | copy-start | bytes 3145732
  7.2 124.0 %all-gather.3.cloned.1.call-start = ((), (), s32[]{:S(2)}) async-start(), calls=%async_computation | async-start | bytes 4210688 | tf_op jit(solution)/shard_map/all_gather | solution.py:145
  142.6 2.3 %copy-start.1 = (bf16[4096,512]{1,0:T(8,128)(2,1)S(1)}, bf16[4096,512]{1,0:T(8,128)(2,1)}, u32[]{:S(2)}) copy-start(bf16[4096,512]{1,0:T(8,128)(2,1)} %param.9) | copy-start | bytes 12582916
Sparse Core Ops, SparseCore 0:
  11.8 119.3 all-gather.2

commit v4 on v1

--- a/solution.py
+++ b/solution.py
@@ -123,6 +123,67 @@
     )(parts)
 
 
+def tensor_kernel(rows_ref, out_ref, got, send, recv, local):
+    n_t = got.shape[0]
+    me = lax.axis_index("dp")
+    mt = lax.axis_index("tensor")
+
+    barrier = pltpu.get_barrier_semaphore()
+
+    def greet(i, carry):
+        q = lax.rem(mt + 1 + i, n_t)
+        pl.semaphore_signal(barrier, 1, device_id=(me, q), device_id_type=MESH)
+        return carry
+
+    lax.fori_loop(0, n_t - 1, greet, 0)
+    pl.semaphore_wait(barrier, n_t - 1)
+
+    def outgoing(q):
+        return pltpu.make_async_remote_copy(
+            src_ref=rows_ref, dst_ref=got.at[mt], send_sem=send.at[q],
+            recv_sem=recv.at[mt], device_id=(me, q), device_id_type=MESH)
+
+    def incoming(q):
+        return pltpu.make_async_remote_copy(
+            src_ref=rows_ref, dst_ref=got.at[q], send_sem=send.at[q],
+            recv_sem=recv.at[q], device_id=(me, q), device_id_type=MESH)
+
+    def start(i, carry):
+        outgoing(lax.rem(mt + 1 + i, n_t)).start()
+        return carry
+
+    lax.fori_loop(0, n_t - 1, start, 0)
+    own = pltpu.make_async_copy(rows_ref, got.at[mt], local.at[0])
+    own.start()
+
+    def finish(i, carry):
+        q = lax.rem(mt + 1 + i, n_t)
+        incoming(q).wait_recv()
+        outgoing(q).wait_send()
+        return carry
+
+    lax.fori_loop(0, n_t - 1, finish, 0)
+    own.wait()
+    out_ref[...] = got[...]
+
+
+def gather_tensor(rows, n_t):
+    k, width = rows.shape
+    return pl.pallas_call(
+        tensor_kernel,
+        out_shape=jax.ShapeDtypeStruct((n_t, k, width), rows.dtype),
+        in_specs=[pl.BlockSpec(memory_space=pltpu.VMEM)],
+        out_specs=pl.BlockSpec(memory_space=pltpu.VMEM),
+        scratch_shapes=[
+            pltpu.VMEM((n_t, k, width), rows.dtype),
+            pltpu.SemaphoreType.DMA((n_t,)),
+            pltpu.SemaphoreType.DMA((n_t,)),
+            pltpu.SemaphoreType.DMA((1,)),
+        ],
+        compiler_params=pltpu.CompilerParams(collective_id=1, has_side_effects=True),
+    )(rows)
+
+
 def per_device(hidden, gain, head, lengths, offsets, targets, mask):
     seq_count, slot_count = offsets.shape
     slots = seq_count * slot_count
@@ -141,7 +202,7 @@
     picked = jnp.take(flat_hidden, seq_of * maxlen + position, axis=0)
     flat_target = targets.reshape(slots)[idx]
 
-    full_rows = lax.all_gather(picked, "tensor", axis=1, tiled=True)
+    full_rows = gather_tensor(picked, n_t).transpose(1, 0, 2).reshape(k, n_t * picked.shape[1])
     values = full_rows.astype(jnp.float32)
     meansq = jnp.mean(values * values, axis=-1, keepdims=True)
     normed = (values * lax.rsqrt(meansq + 1e-06) * gain).astype(jnp.bfloat16)

time: 125 us -> 114 us (0.912)
  blocking collectives: 42.7 us -> 15 us
  Pallas kernels: 16.8 us -> 29.7 us
  other arithmetic: 5.18 us -> 7.59 us
    all_gather x1 -> x0, blocking collectives: 23 us -> none  [per_device(): full_rows = lax.all_gather(picked, 'tensor', axis=1, tiled=True)]
    pallas_call x0 -> x1, Pallas kernels: none -> 12.9 us  [gather_tensor(): pl.pallas_call(tensor_kernel, out_shape=jax.ShapeDtypeStruct((n_t, k, wid...]
    unnamed x1, blocking collectives: 19.7 us -> 15 us
where the time goes in v4:
time: 114 us
  waiting for transfers between devices  34.7 us (30%)
  Pallas kernels  29.7 us (26%)
  between operations  15.5 us (14%)
  blocking collectives  15 us (13%)
  other arithmetic  7.59 us (7%)
  matrix products  5.85 us (5%)
  local copies, waits for them, and re-layouts  5.16 us (5%)
    all_gather x1, waiting for transfers between devices, per_device(): rows_piece = lax.all_gather(normed, 'dp', axis=0, tiled=True)  34.7 us
    pallas_call x1, Pallas kernels, exchange_stats(): pl.pallas_call(stats_kernel, out_shape=jax.ShapeDtypeStruct((four, k), jn...  16.8 us
    unnamed x1, blocking collectives  15 us
    pallas_call x1, Pallas kernels, gather_tensor(): pl.pallas_call(tensor_kernel, out_shape=jax.ShapeDtypeStruct((n_t, k, wid...  12.9 us
    dot_general x1, matrix products, per_device(): logits = jnp.dot(rows_piece, head, preferred_element_type=jnp.float32)  5.85 us
  transfers between devices with their start and end apart: 1, of which 1 were waited for; matrix products, arithmetic and copies ran while one was open for 2% of the time, Pallas kernels for 0%

profile of v4, /device:TPU:1, one launch (start us, length us, event | category | flops | bytes accessed | tf_op | source)
XLA Modules:
  0.0 113.6 jit_solution(3466405869229115543)
XLA Ops:
  7.2 0.0 copy-start
  7.2 0.0 all-gather.3.cloned.1.call-start
  8.0 0.7 compare_bitcast_fusion
  8.6 0.1 copy.16
  8.7 0.1 reduce-window.8
  8.8 0.1 add_reduce_fusion
  8.9 0.1 select_reduce_fusion.3
  9.0 1.3 %gather_fusion = s32[16]{0:T(128)S(1)} fusion(s32[32]{0:T(128)} %bitcast.47, s32[1024]{0:T(1024)S(1)} %pad_clamp_fusion.1), kind=kCustom, calls=%fused_computation | custom fusion | bytes 192 | tf_op jit(solution)/shard_map/gather | solution.py:200
  10.4 0.0 copy-done
  10.4 0.6 gather_fusion.1
  11.0 0.7 broadcast_select_fusion.rows_ref
  11.7 12.9 %shard_map.86 = bf16[8,16,512]{2,1,0:T(8,128)(2,1)} custom-call(bf16[16,512]{1,0:T(8,128)(2,1)} %broadcast_select_fusion.rows_ref), custom_call_target="tpu_custom_call" | custom-call | tf_op jit(solution)/shard_map/pallas_call | solution.py:172
  24.6 1.1 fusion.1
  25.7 0.9 convert_bitcast_fusion
  26.6 1.5 %multiply_convert_fusion = bf16[16,4096]{1,0:T(8,128)(2,1)} fusion(f32[16,4096]{1,0:T(8,128)S(1)} %bitcast.49, f32[4096]{0:T(1024)} %param.8, f32[16]{0:T(128)S(1)} %add_rsqrt_fusion), kind=kLoop, calls=%fused_computation.11 | loop fusion | flops 196608 | bytes 409664 | tf_op jit(solution)/shard_map/convert_element_type | solution.py:208
  28.1 0.0 all-gather.3.cloned.1.call-update
  28.1 1.3 %gather_fusion.2 = s32[16]{0:T(128)S(1)} fusion(s32[32]{0:T(128)} %bitcast.48, s32[1024]{0:T(1024)S(1)} %pad_clamp_fusion.1), kind=kCustom, calls=%fused_computation.2 | custom fusion | bytes 192 | tf_op jit(solution)/shard_map/gather | solution.py:203
  29.4 1.3 %dynamic-slice = u32[1]{0:T(128)} dynamic-slice(u32[256]{0:T(256)} %constant.75, u32[]{:T(128)S(6)} %add.94), dynamic_slice_sizes={1} | dynamic-slice | bytes 12
  31.4 0.2 dynamic-update-slice
  31.6 15.0 %all-reduce = s32[512]{0:T(512)S(1)} all-reduce(s32[512]{0:T(512)S(1)} %dynamic-update-slice), channel_id=2, replica_groups=mesh['dp'=32,'tensor'=8] {'dp'}, use_global_device_ids=true, to_apply=%add | all-reduce | flops 512 | bytes 4096
  46.6 34.7 %all-gather.3.cloned.1.call-done = bf16[512,4096]{1,0:T(8,128)(2,1)} async-done(((bf16[16,4096]{1,0:T(8,128)(2,1)}), bf16[512,4096]{1,0:T(8,128)(2,1)}) %all-gather.3.cloned.1.call-update) | async-done | bytes 4194320 | tf_op jit(solution)/shard_map/all_gather | solution.py:213
  81.3 5.8 %fusion.6 = (f32[512]{0:T(512)S(1)}, f32[512,512]{0,1:T(8,128)S(1)}) fusion(bf16[512,4096]{1,0:T(8,128)(2,1)} %all-gather.3.cloned.1.call-done, bf16[4096,512]{1,0:T(8,128)(2,1)} %param.9), kind=kOutput, calls=%fused_computation.46 | convolution fusion | flops 2147745280 | bytes 9439232 | tf_op jit(solution)/shard_map/dot_general | solution.py:215
  87.2 0.1 stack.15
  87.2 0.3 fusion
  87.6 0.1 stack.16
  87.7 0.1 stack.17
  87.8 0.1 stack.18
  87.8 0.7 maximum_bitcast_fusion.part_ref
  88.5 16.8 %shard_map.87 = f32[4,16]{1,0:T(4,128)} custom-call(f32[32,4,16]{2,1,0:T(4,128)} %maximum_bitcast_fusion.part_ref), custom_call_target="tpu_custom_call" | custom-call | tf_op jit(solution)/shard_map/pallas_call | solution.py:107
  105.3 0.8 subtract_bitcast_fusion.1
  106.1 0.6 select_reduce_fusion.1
  (9 shorter events, 0.1 us)
Async XLA Ops:
  7.2 3.2 %copy-start = (bf16[1,1024,512]{2,1,0:T(8,128)(2,1)S(1)}, bf16[1,1024,512]{2,1,0:T(8,128)(2,1)}, u32[]{:S(2)}) copy-start(bf16[1,1024,512]{2,1,0:T(8,128)(2,1)} %param.7) | copy-start | bytes 3145732
  7.2 74.1 %all-gather.3.cloned.1.call-start = ((), (), s32[]{:S(2)}) async-start(), calls=%async_computation | async-start | bytes 4325376 | tf_op jit(solution)/shard_map/all_gather | solution.py:213
Sparse Core Ops, SparseCore 0:
  28.2 53.0 all-gather.2

commit v5 on v4

--- a/solution.py
+++ b/solution.py
@@ -184,6 +184,102 @@
     )(rows)
 
 
+def rows_kernel(block_ref, out_ref, send_d, recv_d, send_f, recv_f, send_s, recv_s, local):
+    n_chip = send_d.shape[0]
+    me = lax.axis_index("dp")
+    mt = lax.axis_index("tensor")
+    chip = me // 2
+    core = me % 2
+    sib = me + 1 - 2 * core
+
+    barrier = pltpu.get_barrier_semaphore()
+
+    def greet(i, carry):
+        c = lax.rem(chip + 1 + i, n_chip)
+        pl.semaphore_signal(barrier, 1, device_id=(c * 2 + core, mt), device_id_type=MESH)
+        return carry
+
+    lax.fori_loop(0, n_chip - 1, greet, 0)
+    pl.semaphore_signal(barrier, 1, device_id=(sib, mt), device_id_type=MESH)
+    pl.semaphore_wait(barrier, n_chip)
+
+    def direct(c):
+        return pltpu.make_async_remote_copy(
+            src_ref=block_ref, dst_ref=out_ref.at[me], send_sem=send_d.at[c],
+            recv_sem=recv_d.at[chip], device_id=(c * 2 + core, mt), device_id_type=MESH)
+
+    def direct_in(c):
+        return pltpu.make_async_remote_copy(
+            src_ref=block_ref, dst_ref=out_ref.at[c * 2 + core], send_sem=send_d.at[c],
+            recv_sem=recv_d.at[c], device_id=(c * 2 + core, mt), device_id_type=MESH)
+
+    def forward(c):
+        return pltpu.make_async_remote_copy(
+            src_ref=out_ref.at[c * 2 + core], dst_ref=out_ref.at[c * 2 + core], send_sem=send_f.at[c],
+            recv_sem=recv_f.at[c], device_id=(sib, mt), device_id_type=MESH)
+
+    def forward_in(c):
+        return pltpu.make_async_remote_copy(
+            src_ref=out_ref.at[c * 2 + 1 - core], dst_ref=out_ref.at[c * 2 + 1 - core],
+            send_sem=send_f.at[c], recv_sem=recv_f.at[c], device_id=(sib, mt), device_id_type=MESH)
+
+    to_sib = pltpu.make_async_remote_copy(
+        src_ref=block_ref, dst_ref=out_ref.at[me], send_sem=send_s.at[0],
+        recv_sem=recv_s.at[0], device_id=(sib, mt), device_id_type=MESH)
+    from_sib = pltpu.make_async_remote_copy(
+        src_ref=block_ref, dst_ref=out_ref.at[sib], send_sem=send_s.at[0],
+        recv_sem=recv_s.at[0], device_id=(sib, mt), device_id_type=MESH)
+
+    def start(i, carry):
+        direct(lax.rem(chip + 1 + i, n_chip)).start()
+        return carry
+
+    lax.fori_loop(0, n_chip - 1, start, 0)
+    to_sib.start()
+    own = pltpu.make_async_copy(block_ref, out_ref.at[me], local.at[0])
+    own.start()
+
+    def relay(i, carry):
+        c = lax.rem(chip + n_chip - 1 - i, n_chip)
+        direct_in(c).wait_recv()
+        forward(c).start()
+        return carry
+
+    lax.fori_loop(0, n_chip - 1, relay, 0)
+
+    def finish(i, carry):
+        c = lax.rem(chip + 1 + i, n_chip)
+        forward_in(c).wait_recv()
+        direct(c).wait_send()
+        forward(c).wait_send()
+        return carry
+
+    lax.fori_loop(0, n_chip - 1, finish, 0)
+    from_sib.wait_recv()
+    to_sib.wait_send()
+    own.wait()
+
+
+def gather_rows(block, n_dp):
+    n_chip = n_dp // 2
+    return pl.pallas_call(
+        rows_kernel,
+        out_shape=jax.ShapeDtypeStruct((n_dp,) + block.shape, block.dtype),
+        in_specs=[pl.BlockSpec(memory_space=pltpu.VMEM)],
+        out_specs=pl.BlockSpec(memory_space=pl.ANY),
+        scratch_shapes=[
+            pltpu.SemaphoreType.DMA((n_chip,)),
+            pltpu.SemaphoreType.DMA((n_chip,)),
+            pltpu.SemaphoreType.DMA((n_chip,)),
+            pltpu.SemaphoreType.DMA((n_chip,)),
+            pltpu.SemaphoreType.DMA((1,)),
+            pltpu.SemaphoreType.DMA((1,)),
+            pltpu.SemaphoreType.DMA((1,)),
+        ],
+        compiler_params=pltpu.CompilerParams(collective_id=2, has_side_effects=True),
+    )(block)
+
+
 def per_device(hidden, gain, head, lengths, offsets, targets, mask):
     seq_count, slot_count = offsets.shape
     slots = seq_count * slot_count
@@ -210,8 +306,14 @@
     vocab_width = head.shape[1]
     vocab_start = (lax.axis_index("dp") * n_t + lax.axis_index("tensor")) * vocab_width
     columns = jnp.arange(vocab_width, dtype=jnp.int32)
-    rows_piece = lax.all_gather(normed, "dp", axis=0, tiled=True)
-    target_piece = lax.all_gather(flat_target, "dp", axis=0, tiled=True)
+    width = normed.shape[1]
+    digits = jnp.stack([flat_target // 65536, (flat_target // 256) % 256, flat_target % 256], axis=1)
+    tail = jnp.zeros((k, 128), jnp.bfloat16).at[:, :3].set(digits.astype(jnp.bfloat16))
+    block = jnp.concatenate([normed, tail], axis=1)
+    gathered = gather_rows(block, n_dp).reshape(n_dp * k, width + 128)
+    rows_piece = gathered[:, :width]
+    got_digits = gathered[:, width : width + 3].astype(jnp.int32)
+    target_piece = got_digits[:, 0] * 65536 + got_digits[:, 1] * 256 + got_digits[:, 2]
     logits = jnp.dot(rows_piece, head, preferred_element_type=jnp.float32)
     top = jnp.max(logits, axis=-1)
     expo = jnp.exp(logits - top[:, None])

time: 114 us -> 88.5 us (0.78)
  Pallas kernels: 29.7 us -> 67.1 us
  waiting for transfers between devices: 34.7 us -> 0 us
  blocking collectives: 15 us -> 0 us
  between operations: 15.5 us -> 1.44 us
  other arithmetic: 7.59 us -> 9.04 us
    pallas_call x0 -> x1, Pallas kernels: none -> 37.9 us  [gather_rows(): pl.pallas_call(rows_kernel, out_shape=jax.ShapeDtypeStruct((n_dp,) + bloc...]
    all_gather x1 -> x0, waiting for transfers between devices: 34.7 us -> none  [per_device(): rows_piece = lax.all_gather(normed, 'dp', axis=0, tiled=True)]
    unnamed x1 -> x0, blocking collectives: 15 us -> none
    unnamed x5 -> x3, local copies, waits for them, and re-layouts: 1.52 us -> 0.11 us
    another operation x1 -> x5, other arithmetic: 0.06 us -> 1.38 us
  transfers between devices with their start and end apart: 1 -> 0, of which waited for: 1 -> 0; matrix products, arithmetic and copies ran while one was open for 2% -> 0% of each run, Pallas kernels for 0% -> 0%
where the time goes in v5:
time: 88.5 us; the launch traced here: 88.1 us
  Pallas kernels  67.1 us (76%)
  other arithmetic  9.04 us (10%)
  matrix products  5.85 us (7%)
  local copies, waits for them, and re-layouts  4.76 us (5%)
  between operations  1.44 us (2%)
    pallas_call x1, Pallas kernels, gather_rows(): pl.pallas_call(rows_kernel, out_shape=jax.ShapeDtypeStruct((n_dp,) + bloc...  37.9 us
    pallas_call x1, Pallas kernels, exchange_stats(): pl.pallas_call(stats_kernel, out_shape=jax.ShapeDtypeStruct((four, k), jn...  16.2 us
    pallas_call x1, Pallas kernels, gather_tensor(): pl.pallas_call(tensor_kernel, out_shape=jax.ShapeDtypeStruct((n_t, k, wid...  12.9 us
    dot_general x1, matrix products, per_device(): logits = jnp.dot(rows_piece, head, preferred_element_type=jnp.float32)  5.85 us

profile of v5, /device:TPU:1, one launch (start us, length us, event | category | flops | bytes accessed | tf_op | source)
XLA Modules:
  0.0 88.1 jit_solution(7020297274666610006)
XLA Ops:
  0.6 0.0 copy-start
  0.6 0.7 compare_bitcast_fusion
  1.4 0.1 copy.48
  1.5 0.1 reduce-window.8
  1.5 0.1 add_reduce_fusion
  1.6 0.1 select_reduce_fusion.3
  1.8 1.3 %gather_fusion.2 = s32[16]{0:T(128)S(1)} fusion(s32[32]{0:T(128)} %bitcast.67, s32[1024]{0:T(1024)S(1)} %pad_clamp_fusion.1), kind=kCustom, calls=%fused_computation.2 | custom fusion | bytes 192 | tf_op jit(solution)/shard_map/gather | solution.py:299
  3.2 0.1 copy.50
  3.3 0.6 compare_reduce_fusion
  3.9 0.7 broadcast_select_fusion.1
  4.6 0.0 copy-done
  4.6 1.3 %gather_fusion = s32[16]{0:T(128)S(1)} fusion(s32[32]{0:T(128)} %bitcast.68, s32[1024]{0:T(1024)S(1)} %pad_clamp_fusion.1), kind=kCustom, calls=%fused_computation | custom fusion | bytes 192 | tf_op jit(solution)/shard_map/gather | solution.py:296
  6.6 0.6 gather_fusion.1
  7.2 0.7 broadcast_select_fusion.rows_ref
  7.9 12.9 %shard_map.86 = bf16[8,16,512]{2,1,0:T(8,128)(2,1)} custom-call(bf16[16,512]{1,0:T(8,128)(2,1)} %broadcast_select_fusion.rows_ref), custom_call_target="tpu_custom_call" | custom-call | tf_op jit(solution)/shard_map/pallas_call | solution.py:172
  20.8 0.9 %convert_bitcast_fusion = f32[8,2,8,512]{3,2,1,0:T(8,128)S(1)} fusion(bf16[8,16,512]{2,1,0:T(8,128)(2,1)} %shard_map.86), kind=kLoop, calls=%fused_computation.11 | loop fusion | flops 65536 | bytes 393216
  21.8 1.1 %fusion.4 = f32[16]{0:T(128)S(1)} fusion(bf16[8,16,512]{2,1,0:T(8,128)(2,1)} %shard_map.86), kind=kLoop, calls=%fused_computation.14 | loop fusion | flops 196592 | bytes 131136 | tf_op jit(solution)/shard_map/reduce_sum | solution.py:303
  22.8 0.8 multiply_convert_fusion
  23.6 0.7 fusion.5.block_ref
  24.3 37.9 %shard_map.87 = bf16[32,16,4224]{2,1,0:T(8,128)(2,1)} custom-call(bf16[16,4224]{1,0:T(8,128)(2,1)} %fusion.5.block_ref), custom_call_target="tpu_custom_call" | custom-call | tf_op jit(solution)/shard_map/pallas_call | solution.py:265
  62.2 5.9 %fusion.16 = (f32[512]{0:T(512)S(1)}, f32[512,512]{0,1:T(8,128)S(1)}) fusion(bf16[4096,512]{1,0:T(8,128)(2,1)} %param.11, bf16[512,4224]{1,0:T(8,128)(2,1)} %bitcast.69), kind=kOutput, calls=%fused_computation.75 | convolution fusion | flops 2147745280 | bytes 9439232 | tf_op jit(solution)/shard_map/dot_general | solution.py:317
  68.1 0.9 %slice.43 = bf16[512,3]{1,0:T(8,128)(2,1)S(1)} slice(bf16[512,4224]{1,0:T(8,128)(2,1)} %bitcast.70), slice={[0:512], [4096:4099]} | slice | bytes 6144 | tf_op jit(solution)/shard_map/slice | solution.py:315
  69.0 0.1 copy.56
  69.2 0.3 fusion.2
  69.5 0.1 stack.26
  69.6 0.1 stack.25
  69.7 0.1 stack.24
  69.7 0.1 stack.23
  69.8 0.7 maximum_bitcast_fusion.part_ref
  70.5 16.2 %shard_map.88 = f32[4,16]{1,0:T(4,128)} custom-call(f32[32,4,16]{2,1,0:T(4,128)} %maximum_bitcast_fusion.part_ref), custom_call_target="tpu_custom_call" | custom-call | tf_op jit(solution)/shard_map/pallas_call | solution.py:107
  86.7 0.8 subtract_bitcast_fusion.1
  87.5 0.6 select_reduce_fusion.1
  (11 shorter events, 0.1 us)
Async XLA Ops:
  0.6 3.9 %copy-start = (bf16[1,1024,512]{2,1,0:T(8,128)(2,1)S(1)}, bf16[1,1024,512]{2,1,0:T(8,128)(2,1)}, u32[]{:S(2)}) copy-start(bf16[1,1024,512]{2,1,0:T(8,128)(2,1)} %param.9) | copy-start | bytes 3145732

commit v6 on v5

--- a/solution.py
+++ b/solution.py
@@ -123,7 +123,7 @@
     )(parts)
 
 
-def tensor_kernel(rows_ref, out_ref, got, send, recv, local):
+def tensor_kernel(rows_ref, gain_ref, tail_ref, out_ref, got, send, recv, local):
     n_t = got.shape[0]
     me = lax.axis_index("dp")
     mt = lax.axis_index("tensor")
@@ -164,15 +164,23 @@
 
     lax.fori_loop(0, n_t - 1, finish, 0)
     own.wait()
-    out_ref[...] = got[...]
-
-
-def gather_tensor(rows, n_t):
+
+    width = got.shape[2]
+    values = got[...].astype(jnp.float32)
+    sumsq = jnp.sum(jnp.sum(values * values, axis=0), axis=-1, keepdims=True)
+    scale = lax.rsqrt(sumsq / (n_t * width) + 1e-06)
+    for t in range(n_t):
+        piece = values[t] * scale * gain_ref[pl.ds(t, 1), :]
+        out_ref[:, pl.ds(t * width, width)] = piece.astype(out_ref.dtype)
+    out_ref[:, pl.ds(n_t * width, tail_ref.shape[1])] = tail_ref[...]
+
+
+def normed_block(rows, gain, tail, n_t):
     k, width = rows.shape
     return pl.pallas_call(
         tensor_kernel,
-        out_shape=jax.ShapeDtypeStruct((n_t, k, width), rows.dtype),
-        in_specs=[pl.BlockSpec(memory_space=pltpu.VMEM)],
+        out_shape=jax.ShapeDtypeStruct((k, n_t * width + tail.shape[1]), rows.dtype),
+        in_specs=[pl.BlockSpec(memory_space=pltpu.VMEM)] * 3,
         out_specs=pl.BlockSpec(memory_space=pltpu.VMEM),
         scratch_shapes=[
             pltpu.VMEM((n_t, k, width), rows.dtype),
@@ -181,7 +189,7 @@
             pltpu.SemaphoreType.DMA((1,)),
         ],
         compiler_params=pltpu.CompilerParams(collective_id=1, has_side_effects=True),
-    )(rows)
+    )(rows, gain.reshape(n_t, width), tail)
 
 
 def rows_kernel(block_ref, out_ref, send_d, recv_d, send_f, recv_f, send_s, recv_s, local):
@@ -298,18 +306,13 @@
     picked = jnp.take(flat_hidden, seq_of * maxlen + position, axis=0)
     flat_target = targets.reshape(slots)[idx]
 
-    full_rows = gather_tensor(picked, n_t).transpose(1, 0, 2).reshape(k, n_t * picked.shape[1])
-    values = full_rows.astype(jnp.float32)
-    meansq = jnp.mean(values * values, axis=-1, keepdims=True)
-    normed = (values * lax.rsqrt(meansq + 1e-06) * gain).astype(jnp.bfloat16)
-
     vocab_width = head.shape[1]
     vocab_start = (lax.axis_index("dp") * n_t + lax.axis_index("tensor")) * vocab_width
     columns = jnp.arange(vocab_width, dtype=jnp.int32)
-    width = normed.shape[1]
+    width = n_t * picked.shape[1]
     digits = jnp.stack([flat_target // 65536, (flat_target // 256) % 256, flat_target % 256], axis=1)
     tail = jnp.zeros((k, 128), jnp.bfloat16).at[:, :3].set(digits.astype(jnp.bfloat16))
-    block = jnp.concatenate([normed, tail], axis=1)
+    block = normed_block(picked, gain, tail, n_t)
     gathered = gather_rows(block, n_dp).reshape(n_dp * k, width + 128)
     rows_piece = gathered[:, :width]
     got_digits = gathered[:, width : width + 3].astype(jnp.int32)

time: 88.5 us -> 88.3 us (level)
  other arithmetic: 9.04 us -> 5.49 us
  local copies, waits for them, and re-layouts: 4.76 us -> 7.86 us
    reshape x0 -> x1, local copies, waits for them, and re-layouts: none -> 1.32 us  [normed_block(): gain.reshape(n_t, width)]
    unnamed x3, local copies, waits for them, and re-layouts: 0.11 us -> 1.33 us
    reduce_sum x1 -> x0, other arithmetic: 1.05 us -> none  [per_device(): meansq = jnp.mean(values * values, axis=-1, keepdims=True)]
    unnamed x1 -> x0, other arithmetic: 0.92 us -> none
where the time goes in v6:
time: 88.3 us; the launch traced here: 88 us
  Pallas kernels  67.3 us (76%)
  local copies, waits for them, and re-layouts  7.86 us (9%)
  matrix products  5.85 us (7%)
  other arithmetic  5.49 us (6%)
  between operations  1.41 us (2%)
    pallas_call x1, Pallas kernels, gather_rows(): pl.pallas_call(rows_kernel, out_shape=jax.ShapeDtypeStruct((n_dp,) + bloc...  38.1 us
    pallas_call x1, Pallas kernels, exchange_stats(): pl.pallas_call(stats_kernel, out_shape=jax.ShapeDtypeStruct((four, k), jn...  16.2 us
    pallas_call x1, Pallas kernels, normed_block(): pl.pallas_call(tensor_kernel, out_shape=jax.ShapeDtypeStruct((k, n_t * wi...  13.1 us
    dot_general x1, matrix products, per_device(): logits = jnp.dot(rows_piece, head, preferred_element_type=jnp.float32)  5.85 us

profile of v6, /device:TPU:1, one launch (start us, length us, event | category | flops | bytes accessed | tf_op | source)
XLA Modules:
  0.0 88.0 jit_solution(8656472315038805533)
XLA Ops:
  0.6 0.0 copy-start
  0.6 1.2 %copy-done = bf16[1,1024,512]{2,1,0:T(8,128)(2,1)S(1)} copy-done((bf16[1,1024,512]{2,1,0:T(8,128)(2,1)S(1)}, bf16[1,1024,512]{2,1,0:T(8,128)(2,1)}, u32[]{:S(2)}) %copy-start) | copy-done | bytes 1048600
  1.9 0.7 compare_bitcast_fusion
  2.5 0.1 copy.45
  2.6 0.1 reduce-window.8
  2.7 0.1 add_reduce_fusion
  2.8 0.1 select_reduce_fusion.3
  2.9 1.3 %gather_fusion = s32[16]{0:T(128)S(1)} fusion(s32[32]{0:T(128)} %bitcast.63, s32[1024]{0:T(1024)S(1)} %pad_clamp_fusion.1), kind=kCustom, calls=%fused_computation | custom fusion | bytes 192 | tf_op jit(solution)/shard_map/gather | solution.py:304
  4.9 0.6 gather_fusion.1
  5.5 0.7 broadcast_select_fusion.rows_ref
  6.2 1.3 %reshape.362.gain_ref = f32[8,512]{1,0:T(8,128)} reshape(f32[4096]{0:T(1024)} %param.10) | data formatting | bytes 32768 | tf_op jit(solution)/shard_map/reshape | solution.py:192
  7.5 1.3 %gather_fusion.2 = s32[16]{0:T(128)S(1)} fusion(s32[32]{0:T(128)} %bitcast.64, s32[1024]{0:T(1024)S(1)} %pad_clamp_fusion.1), kind=kCustom, calls=%fused_computation.2 | custom fusion | bytes 192 | tf_op jit(solution)/shard_map/gather | solution.py:307
  8.9 0.1 copy.46
  9.0 0.6 compare_reduce_fusion
  9.6 0.7 broadcast_select_fusion.1
  10.3 0.6 scatter.4.tail_ref
  10.9 13.1 %shard_map.86.block_ref = bf16[16,4224]{1,0:T(8,128)(2,1)} custom-call(bf16[16,512]{1,0:T(8,128)(2,1)} %broadcast_select_fusion.rows_ref, f32[8,512]{1,0:T(8,128)} %reshape.362.gain_ref, bf16[16,128]{1,0:T(8,128)(2,1)} %scatter.4.tail_ref), custom_call_target="tpu_custom_call" | custom-call | tf_op jit(solution)/shard_map/pallas_call | solution.py:180
  24.0 38.1 %shard_map.87 = bf16[32,16,4224]{2,1,0:T(8,128)(2,1)} custom-call(bf16[16,4224]{1,0:T(8,128)(2,1)} %shard_map.86.block_ref), custom_call_target="tpu_custom_call" | custom-call | tf_op jit(solution)/shard_map/pallas_call | solution.py:273
  62.0 5.9 %fusion.13 = (f32[512]{0:T(512)S(1)}, f32[512,512]{0,1:T(8,128)S(1)}) fusion(bf16[4096,512]{1,0:T(8,128)(2,1)} %param.11, bf16[512,4224]{1,0:T(8,128)(2,1)} %bitcast.65), kind=kOutput, calls=%fused_computation.67 | convolution fusion | flops 2147745280 | bytes 9439232 | tf_op jit(solution)/shard_map/dot_general | solution.py:320
  67.9 0.9 %slice.43 = bf16[512,3]{1,0:T(8,128)(2,1)S(1)} slice(bf16[512,4224]{1,0:T(8,128)(2,1)} %bitcast.66), slice={[0:512], [4096:4099]} | slice | bytes 6144 | tf_op jit(solution)/shard_map/slice | solution.py:318
  68.8 0.1 copy.52
  69.0 0.3 fusion.2
  69.3 0.1 stack.26
  69.4 0.1 stack.25
  69.5 0.1 stack.24
  69.5 0.1 stack.23
  69.6 0.7 maximum_bitcast_fusion.part_ref
  70.3 16.2 %shard_map.88 = f32[4,16]{1,0:T(4,128)} custom-call(f32[32,4,16]{2,1,0:T(4,128)} %maximum_bitcast_fusion.part_ref), custom_call_target="tpu_custom_call" | custom-call | tf_op jit(solution)/shard_map/pallas_call | solution.py:107
  86.5 0.8 subtract_bitcast_fusion.1
  87.4 0.6 select_reduce_fusion.1
  (9 shorter events, 0.1 us)
Async XLA Ops:
  0.6 1.2 %copy-start = (bf16[1,1024,512]{2,1,0:T(8,128)(2,1)S(1)}, bf16[1,1024,512]{2,1,0:T(8,128)(2,1)}, u32[]{:S(2)}) copy-start(bf16[1,1024,512]{2,1,0:T(8,128)(2,1)} %param.9) | copy-start | bytes 3145732

commit v7 on v4

--- a/solution.py
+++ b/solution.py
@@ -9,6 +9,7 @@
 
 MESH = pl.DeviceIdType.MESH
 LIVE = 16
+RING = 4
 
 
 def merge(parts):
@@ -184,6 +185,110 @@
     )(rows)
 
 
+def rows_kernel(block_ref, out_ref, send, recv, local):
+    n_dp = out_ref.shape[0]
+    n_chip = n_dp // 2
+    me = lax.axis_index("dp")
+    mt = lax.axis_index("tensor")
+    chip = me // 2
+    core = me % 2
+    x = chip % RING
+    y = chip // RING
+    ua = x + (y - x) * core
+    ub = y + (x - y) * core
+    sib = me + 1 - 2 * core
+
+    def slot(a, b, parity):
+        a = (a + 2 * RING) % RING
+        b = (b + 2 * RING) % RING
+        xx = a + (b - a) * core
+        yy = b + (a - b) * core
+        return (yy * RING + xx) * 2 + parity
+
+    def dev(a, b):
+        return (slot(a, b, core), mt)
+
+    plus_a, minus_a = dev(ua + 1, ub), dev(ua - 1, ub)
+    plus_b, minus_b = dev(ua, ub + 1), dev(ua, ub - 1)
+    sib_dev = (sib, mt)
+
+    barrier = pltpu.get_barrier_semaphore()
+    for target in (plus_a, minus_a, plus_b, minus_b, sib_dev):
+        pl.semaphore_signal(barrier, 1, device_id=target, device_id_type=MESH)
+    pl.semaphore_wait(barrier, 5)
+
+    sends = []
+
+    def put(src_slot, dst_slot, target):
+        src = block_ref if src_slot is None else out_ref.at[src_slot]
+        copy = pltpu.make_async_remote_copy(
+            src_ref=src, dst_ref=out_ref.at[dst_slot], send_sem=send.at[len(sends)],
+            recv_sem=recv.at[dst_slot], device_id=target, device_id_type=MESH)
+        copy.start()
+        sends.append(copy)
+
+    def arrive(dst_slot):
+        pltpu.make_async_remote_copy(
+            src_ref=block_ref, dst_ref=out_ref.at[dst_slot], send_sem=send.at[0],
+            recv_sem=recv.at[dst_slot], device_id=sib_dev, device_id_type=MESH).wait_recv()
+
+    own = pltpu.make_async_copy(block_ref, out_ref.at[me], local.at[0])
+    own.start()
+    for target in (plus_a, minus_a, plus_b, minus_b, sib_dev):
+        put(None, me, target)
+
+    left, right, far = slot(ua - 1, ub, core), slot(ua + 1, ub, core), slot(ua + 2, ub, core)
+    arrive(left)
+    for target in (plus_b, minus_b, sib_dev):
+        put(left, left, target)
+    arrive(right)
+    for target in (plus_b, minus_b, sib_dev):
+        put(right, right, target)
+    pick = 1 - (ua + 3 + core) % 2
+    fwd = pick * left + (1 - pick) * right
+    fwd_dev = (pick * plus_a[0] + (1 - pick) * minus_a[0], mt)
+    put(fwd, fwd, fwd_dev)
+    arrive(far)
+    for target in (plus_b, minus_b, sib_dev):
+        put(far, far, target)
+
+    pick_b = 1 - (ub + 3 + core) % 2
+    for d in (0, -1, 1, 2):
+        lo, hi = slot(ua + d, ub - 1, core), slot(ua + d, ub + 1, core)
+        arrive(lo)
+        put(lo, lo, sib_dev)
+        arrive(hi)
+        put(hi, hi, sib_dev)
+        fwd = pick_b * lo + (1 - pick_b) * hi
+        fwd_dev = (pick_b * plus_b[0] + (1 - pick_b) * minus_b[0], mt)
+        put(fwd, fwd, fwd_dev)
+    for d in (0, -1, 1, 2):
+        far_b = slot(ua + d, ub + 2, core)
+        arrive(far_b)
+        put(far_b, far_b, sib_dev)
+
+    for c in range(n_chip):
+        arrive(c * 2 + 1 - core)
+    for copy in sends:
+        copy.wait_send()
+    own.wait()
+
+
+def gather_rows(block, n_dp):
+    return pl.pallas_call(
+        rows_kernel,
+        out_shape=jax.ShapeDtypeStruct((n_dp,) + block.shape, block.dtype),
+        in_specs=[pl.BlockSpec(memory_space=pltpu.VMEM)],
+        out_specs=pl.BlockSpec(memory_space=pl.ANY),
+        scratch_shapes=[
+            pltpu.SemaphoreType.DMA((n_dp,)),
+            pltpu.SemaphoreType.DMA((n_dp,)),
+            pltpu.SemaphoreType.DMA((1,)),
+        ],
+        compiler_params=pltpu.CompilerParams(collective_id=2, has_side_effects=True),
+    )(block)
+
+
 def per_device(hidden, gain, head, lengths, offsets, targets, mask):
     seq_count, slot_count = offsets.shape
     slots = seq_count * slot_count
@@ -210,8 +315,14 @@
     vocab_width = head.shape[1]
     vocab_start = (lax.axis_index("dp") * n_t + lax.axis_index("tensor")) * vocab_width
     columns = jnp.arange(vocab_width, dtype=jnp.int32)
-    rows_piece = lax.all_gather(normed, "dp", axis=0, tiled=True)
-    target_piece = lax.all_gather(flat_target, "dp", axis=0, tiled=True)
+    width = normed.shape[1]
+    digits = jnp.stack([flat_target // 65536, (flat_target // 256) % 256, flat_target % 256], axis=1)
+    tail = jnp.zeros((k, 128), jnp.bfloat16).at[:, :3].set(digits.astype(jnp.bfloat16))
+    block = jnp.concatenate([normed, tail], axis=1)
+    gathered = gather_rows(block, n_dp).reshape(n_dp * k, width + 128)
+    rows_piece = gathered[:, :width]
+    got_digits = gathered[:, width : width + 3].astype(jnp.int32)
+    target_piece = got_digits[:, 0] * 65536 + got_digits[:, 1] * 256 + got_digits[:, 2]
     logits = jnp.dot(rows_piece, head, preferred_element_type=jnp.float32)
     top = jnp.max(logits, axis=-1)
     expo = jnp.exp(logits - top[:, None])

time: 114 us -> 79.2 us (0.69)
  waiting for transfers between devices: 34.7 us -> 0 us
  Pallas kernels: 29.7 us -> 57.8 us
  blocking collectives: 15 us -> 0 us
  between operations: 15.5 us -> 1.44 us
  other arithmetic: 7.59 us -> 9.04 us
    all_gather x1 -> x0, waiting for transfers between devices: 34.7 us -> none  [per_device(): rows_piece = lax.all_gather(normed, 'dp', axis=0, tiled=True)]
    pallas_call x0 -> x1, Pallas kernels: none -> 30.6 us  [gather_rows(): pl.pallas_call(rows_kernel, out_shape=jax.ShapeDtypeStruct((n_dp,) + bloc...]
    unnamed x1 -> x0, blocking collectives: 15 us -> none
    pallas_call x1, Pallas kernels: 16.8 us -> 14.2 us  [exchange_stats(): pl.pallas_call(stats_kernel, out_shape=jax.ShapeDtypeStruct((four, k), jn...]
    unnamed x5 -> x3, local copies, waits for them, and re-layouts: 1.52 us -> 0.11 us
    another operation x1 -> x5, other arithmetic: 0.06 us -> 1.38 us
  transfers between devices with their start and end apart: 1 -> 0, of which waited for: 1 -> 0; matrix products, arithmetic and copies ran while one was open for 2% -> 0% of each run, Pallas kernels for 0% -> 0%
where the time goes in v7:
time: 79.2 us; the launch traced here: 78.9 us
  Pallas kernels  57.8 us (73%)
  other arithmetic  9.04 us (11%)
  matrix products  5.85 us (7%)
  local copies, waits for them, and re-layouts  4.76 us (6%)
  between operations  1.44 us (2%)
    pallas_call x1, Pallas kernels, gather_rows(): pl.pallas_call(rows_kernel, out_shape=jax.ShapeDtypeStruct((n_dp,) + bloc...  30.6 us
    pallas_call x1, Pallas kernels, exchange_stats(): pl.pallas_call(stats_kernel, out_shape=jax.ShapeDtypeStruct((four, k), jn...  14.2 us
    pallas_call x1, Pallas kernels, gather_tensor(): pl.pallas_call(tensor_kernel, out_shape=jax.ShapeDtypeStruct((n_t, k, wid...  12.9 us
    dot_general x1, matrix products, per_device(): logits = jnp.dot(rows_piece, head, preferred_element_type=jnp.float32)  5.85 us

profile of v7, /device:TPU:1, one launch (start us, length us, event | category | flops | bytes accessed | tf_op | source)
XLA Modules:
  0.0 78.9 jit_solution(11820249303715879184)
XLA Ops:
  0.6 0.0 copy-start
  0.6 0.7 compare_bitcast_fusion
  1.4 0.1 copy.48
  1.5 0.1 reduce-window.8
  1.5 0.1 add_reduce_fusion
  1.6 0.1 select_reduce_fusion.3
  1.8 1.3 %gather_fusion.2 = s32[16]{0:T(128)S(1)} fusion(s32[32]{0:T(128)} %bitcast.67, s32[1024]{0:T(1024)S(1)} %pad_clamp_fusion.1), kind=kCustom, calls=%fused_computation.2 | custom fusion | bytes 192 | tf_op jit(solution)/shard_map/gather | solution.py:308
  3.2 0.1 copy.50
  3.3 0.6 compare_reduce_fusion
  3.9 0.7 broadcast_select_fusion.1
  4.6 0.0 copy-done
  4.6 1.3 %gather_fusion = s32[16]{0:T(128)S(1)} fusion(s32[32]{0:T(128)} %bitcast.68, s32[1024]{0:T(1024)S(1)} %pad_clamp_fusion.1), kind=kCustom, calls=%fused_computation | custom fusion | bytes 192 | tf_op jit(solution)/shard_map/gather | solution.py:305
  6.6 0.6 gather_fusion.1
  7.2 0.7 broadcast_select_fusion.rows_ref
  7.9 12.9 %shard_map.86 = bf16[8,16,512]{2,1,0:T(8,128)(2,1)} custom-call(bf16[16,512]{1,0:T(8,128)(2,1)} %broadcast_select_fusion.rows_ref), custom_call_target="tpu_custom_call" | custom-call | tf_op jit(solution)/shard_map/pallas_call | solution.py:173
  20.8 0.9 %convert_bitcast_fusion = f32[8,2,8,512]{3,2,1,0:T(8,128)S(1)} fusion(bf16[8,16,512]{2,1,0:T(8,128)(2,1)} %shard_map.86), kind=kLoop, calls=%fused_computation.11 | loop fusion | flops 65536 | bytes 393216
  21.8 1.1 %fusion.4 = f32[16]{0:T(128)S(1)} fusion(bf16[8,16,512]{2,1,0:T(8,128)(2,1)} %shard_map.86), kind=kLoop, calls=%fused_computation.14 | loop fusion | flops 196592 | bytes 131136 | tf_op jit(solution)/shard_map/reduce_sum | solution.py:312
  22.8 0.8 %multiply_convert_fusion = bf16[16,4096]{1,0:T(8,128)(2,1)S(1)} fusion(f32[16,4096]{1,0:T(8,128)S(1)} %bitcast.71, f32[4096]{0:T(1024)} %param.10, f32[16]{0:T(128)S(1)} %add_rsqrt_fusion), kind=kLoop, calls=%fused_computation.15 | loop fusion | flops 196608 | bytes 409664 | tf_op jit(solution)/shard_map/convert_element_type | solution.py:313
  23.6 0.7 fusion.5.block_ref
  24.3 30.6 %shard_map.87 = bf16[32,16,4224]{2,1,0:T(8,128)(2,1)} custom-call(bf16[16,4224]{1,0:T(8,128)(2,1)} %fusion.5.block_ref), custom_call_target="tpu_custom_call" | custom-call | tf_op jit(solution)/shard_map/pallas_call | solution.py:278
  54.9 5.9 %fusion.16 = (f32[512]{0:T(512)S(1)}, f32[512,512]{0,1:T(8,128)S(1)}) fusion(bf16[4096,512]{1,0:T(8,128)(2,1)} %param.11, bf16[512,4224]{1,0:T(8,128)(2,1)} %bitcast.69), kind=kOutput, calls=%fused_computation.75 | convolution fusion | flops 2147745280 | bytes 9439232 | tf_op jit(solution)/shard_map/dot_general | solution.py:326
  60.8 0.9 %slice.43 = bf16[512,3]{1,0:T(8,128)(2,1)S(1)} slice(bf16[512,4224]{1,0:T(8,128)(2,1)} %bitcast.70), slice={[0:512], [4096:4099]} | slice | bytes 6144 | tf_op jit(solution)/shard_map/slice | solution.py:324
  61.7 0.1 copy.56
  61.8 0.3 fusion.2
  62.2 0.1 stack.26
  62.3 0.1 stack.25
  62.4 0.1 stack.24
  62.4 0.1 stack.23
  62.5 0.7 maximum_bitcast_fusion.part_ref
  63.2 14.2 %shard_map.88 = f32[4,16]{1,0:T(4,128)} custom-call(f32[32,4,16]{2,1,0:T(4,128)} %maximum_bitcast_fusion.part_ref), custom_call_target="tpu_custom_call" | custom-call | tf_op jit(solution)/shard_map/pallas_call | solution.py:108
  77.4 0.8 %subtract_bitcast_fusion.1 = (f32[16]{0:T(128)S(1)}, f32[16]{0:T(128)S(1)}) fusion(f32[4,16]{1,0:T(4,128)} %shard_map.88), kind=kLoop, calls=%fused_computation.71 | loop fusion | flops 64 | bytes 384 | tf_op jit(solution)/shard_map/sub | solution.py:337
  78.2 0.6 select_reduce_fusion.1
  (11 shorter events, 0.1 us)
Async XLA Ops:
  0.6 3.9 %copy-start = (bf16[1,1024,512]{2,1,0:T(8,128)(2,1)S(1)}, bf16[1,1024,512]{2,1,0:T(8,128)(2,1)}, u32[]{:S(2)}) copy-start(bf16[1,1024,512]{2,1,0:T(8,128)(2,1)} %param.9) | copy-start | bytes 3145732

commit v8 on v7

--- a/solution.py
+++ b/solution.py
@@ -124,68 +124,7 @@
     )(parts)
 
 
-def tensor_kernel(rows_ref, out_ref, got, send, recv, local):
-    n_t = got.shape[0]
-    me = lax.axis_index("dp")
-    mt = lax.axis_index("tensor")
-
-    barrier = pltpu.get_barrier_semaphore()
-
-    def greet(i, carry):
-        q = lax.rem(mt + 1 + i, n_t)
-        pl.semaphore_signal(barrier, 1, device_id=(me, q), device_id_type=MESH)
-        return carry
-
-    lax.fori_loop(0, n_t - 1, greet, 0)
-    pl.semaphore_wait(barrier, n_t - 1)
-
-    def outgoing(q):
-        return pltpu.make_async_remote_copy(
-            src_ref=rows_ref, dst_ref=got.at[mt], send_sem=send.at[q],
-            recv_sem=recv.at[mt], device_id=(me, q), device_id_type=MESH)
-
-    def incoming(q):
-        return pltpu.make_async_remote_copy(
-            src_ref=rows_ref, dst_ref=got.at[q], send_sem=send.at[q],
-            recv_sem=recv.at[q], device_id=(me, q), device_id_type=MESH)
-
-    def start(i, carry):
-        outgoing(lax.rem(mt + 1 + i, n_t)).start()
-        return carry
-
-    lax.fori_loop(0, n_t - 1, start, 0)
-    own = pltpu.make_async_copy(rows_ref, got.at[mt], local.at[0])
-    own.start()
-
-    def finish(i, carry):
-        q = lax.rem(mt + 1 + i, n_t)
-        incoming(q).wait_recv()
-        outgoing(q).wait_send()
-        return carry
-
-    lax.fori_loop(0, n_t - 1, finish, 0)
-    own.wait()
-    out_ref[...] = got[...]
-
-
-def gather_tensor(rows, n_t):
-    k, width = rows.shape
-    return pl.pallas_call(
-        tensor_kernel,
-        out_shape=jax.ShapeDtypeStruct((n_t, k, width), rows.dtype),
-        in_specs=[pl.BlockSpec(memory_space=pltpu.VMEM)],
-        out_specs=pl.BlockSpec(memory_space=pltpu.VMEM),
-        scratch_shapes=[
-            pltpu.VMEM((n_t, k, width), rows.dtype),
-            pltpu.SemaphoreType.DMA((n_t,)),
-            pltpu.SemaphoreType.DMA((n_t,)),
-            pltpu.SemaphoreType.DMA((1,)),
-        ],
-        compiler_params=pltpu.CompilerParams(collective_id=1, has_side_effects=True),
-    )(rows)
-
-
-def rows_kernel(block_ref, out_ref, send, recv, local):
+def rows_kernel(rows_ref, gain_ref, target_ref, out_ref, got, block_ref, send_t, recv_t, send, recv, local):
     n_dp = out_ref.shape[0]
     n_chip = n_dp // 2
     me = lax.axis_index("dp")
@@ -212,10 +151,58 @@
     plus_b, minus_b = dev(ua, ub + 1), dev(ua, ub - 1)
     sib_dev = (sib, mt)
 
+    n_t = got.shape[0]
     barrier = pltpu.get_barrier_semaphore()
     for target in (plus_a, minus_a, plus_b, minus_b, sib_dev):
         pl.semaphore_signal(barrier, 1, device_id=target, device_id_type=MESH)
-    pl.semaphore_wait(barrier, 5)
+
+    def greet(i, carry):
+        q = lax.rem(mt + 1 + i, n_t)
+        pl.semaphore_signal(barrier, 1, device_id=(me, q), device_id_type=MESH)
+        return carry
+
+    lax.fori_loop(0, n_t - 1, greet, 0)
+    pl.semaphore_wait(barrier, 5 + n_t - 1)
+
+    def t_out(q):
+        return pltpu.make_async_remote_copy(
+            src_ref=rows_ref, dst_ref=got.at[mt], send_sem=send_t.at[q],
+            recv_sem=recv_t.at[mt], device_id=(me, q), device_id_type=MESH)
+
+    def t_in(q):
+        return pltpu.make_async_remote_copy(
+            src_ref=rows_ref, dst_ref=got.at[q], send_sem=send_t.at[q],
+            recv_sem=recv_t.at[q], device_id=(me, q), device_id_type=MESH)
+
+    def t_start(i, carry):
+        t_out(lax.rem(mt + 1 + i, n_t)).start()
+        return carry
+
+    lax.fori_loop(0, n_t - 1, t_start, 0)
+    own_t = pltpu.make_async_copy(rows_ref, got.at[mt], local.at[1])
+    own_t.start()
+
+    def t_finish(i, carry):
+        q = lax.rem(mt + 1 + i, n_t)
+        t_in(q).wait_recv()
+        t_out(q).wait_send()
+        return carry
+
+    lax.fori_loop(0, n_t - 1, t_finish, 0)
+    own_t.wait()
+
+    width = got.shape[2]
+    values = got[...].astype(jnp.float32)
+    sumsq = jnp.sum(jnp.sum(values * values, axis=0), axis=-1, keepdims=True)
+    scale = lax.rsqrt(sumsq / (n_t * width) + 1e-06)
+    for t in range(n_t):
+        piece = values[t] * scale * gain_ref[:, pl.ds(t * width, width)]
+        block_ref[:, pl.ds(t * width, width)] = piece.astype(block_ref.dtype)
+    tgt = target_ref[...]
+    lane = lax.broadcasted_iota(jnp.int32, (tgt.shape[0], 128), 1)
+    tail = jnp.where(lane == 0, tgt // 65536, jnp.where(lane == 1, (tgt // 256) % 256,
+                                                          jnp.where(lane == 2, tgt % 256, 0)))
+    block_ref[:, pl.ds(n_t * width, 128)] = tail.astype(jnp.float32).astype(block_ref.dtype)
 
     sends = []
 
@@ -274,19 +261,25 @@
     own.wait()
 
 
-def gather_rows(block, n_dp):
+def gather_rows(rows, gain, target, n_dp, n_t):
+    k, width = rows.shape
+    shape = (k, n_t * width + 128)
     return pl.pallas_call(
         rows_kernel,
-        out_shape=jax.ShapeDtypeStruct((n_dp,) + block.shape, block.dtype),
-        in_specs=[pl.BlockSpec(memory_space=pltpu.VMEM)],
+        out_shape=jax.ShapeDtypeStruct((n_dp,) + shape, rows.dtype),
+        in_specs=[pl.BlockSpec(memory_space=pltpu.VMEM)] * 3,
         out_specs=pl.BlockSpec(memory_space=pl.ANY),
         scratch_shapes=[
+            pltpu.VMEM((n_t, k, width), rows.dtype),
+            pltpu.VMEM(shape, rows.dtype),
+            pltpu.SemaphoreType.DMA((n_t,)),
+            pltpu.SemaphoreType.DMA((n_t,)),
             pltpu.SemaphoreType.DMA((n_dp,)),
             pltpu.SemaphoreType.DMA((n_dp,)),
-            pltpu.SemaphoreType.DMA((1,)),
+            pltpu.SemaphoreType.DMA((2,)),
         ],
         compiler_params=pltpu.CompilerParams(collective_id=2, has_side_effects=True),
-    )(block)
+    )(rows, gain.reshape(1, n_t * width), target.reshape(k, 1))
 
 
 def per_device(hidden, gain, head, lengths, offsets, targets, mask):
@@ -307,19 +300,11 @@
     picked = jnp.take(flat_hidden, seq_of * maxlen + position, axis=0)
     flat_target = targets.reshape(slots)[idx]
 
-    full_rows = gather_tensor(picked, n_t).transpose(1, 0, 2).reshape(k, n_t * picked.shape[1])
-    values = full_rows.astype(jnp.float32)
-    meansq = jnp.mean(values * values, axis=-1, keepdims=True)
-    normed = (values * lax.rsqrt(meansq + 1e-06) * gain).astype(jnp.bfloat16)
-
     vocab_width = head.shape[1]
     vocab_start = (lax.axis_index("dp") * n_t + lax.axis_index("tensor")) * vocab_width
     columns = jnp.arange(vocab_width, dtype=jnp.int32)
-    width = normed.shape[1]
-    digits = jnp.stack([flat_target // 65536, (flat_target // 256) % 256, flat_target % 256], axis=1)
-    tail = jnp.zeros((k, 128), jnp.bfloat16).at[:, :3].set(digits.astype(jnp.bfloat16))
-    block = jnp.concatenate([normed, tail], axis=1)
-    gathered = gather_rows(block, n_dp).reshape(n_dp * k, width + 128)
+    width = n_t * picked.shape[1]
+    gathered = gather_rows(picked, gain, flat_target, n_dp, n_t).reshape(n_dp * k, width + 128)
     rows_piece = gathered[:, :width]
     got_digits = gathered[:, width : width + 3].astype(jnp.int32)
     target_piece = got_digits[:, 0] * 65536 + got_digits[:, 1] * 256 + got_digits[:, 2]

time: 79.2 us -> 73 us (0.922)
  other arithmetic: 9.04 us -> 4.17 us
  Pallas kernels: 57.8 us -> 54.7 us
  local copies, waits for them, and re-layouts: 4.76 us -> 6.54 us
    pallas_call x2 -> x1, Pallas kernels: 43.6 us -> 40.8 us  [gather_rows(): pl.pallas_call(rows_kernel, out_shape=jax.ShapeDtypeStruct((n_dp,) + shap...]
    another operation x5 -> x1, other arithmetic: 1.38 us -> 0.06 us
    unnamed x3, local copies, waits for them, and re-layouts: 0.11 us -> 1.33 us
    reduce_sum x1 -> x0, other arithmetic: 1.05 us -> none  [per_device(): meansq = jnp.mean(values * values, axis=-1, keepdims=True)]
    unnamed x1 -> x0, other arithmetic: 0.92 us -> none
    convert_element_type x1 -> x0, other arithmetic: 0.82 us -> none  [per_device(): normed = (values * lax.rsqrt(meansq + 1e-06) * gain).astype(jnp.bfloat16)]
where the time goes in v8:
time: 73 us; the launch traced here: 72.7 us
  Pallas kernels  54.7 us (75%)
  local copies, waits for them, and re-layouts  6.54 us (9%)
  matrix products  5.85 us (8%)
  other arithmetic  4.17 us (6%)
  between operations  1.38 us (2%)
    pallas_call x1, Pallas kernels, gather_rows(): pl.pallas_call(rows_kernel, out_shape=jax.ShapeDtypeStruct((n_dp,) + shap...  40.8 us
    pallas_call x1, Pallas kernels, exchange_stats(): pl.pallas_call(stats_kernel, out_shape=jax.ShapeDtypeStruct((four, k), jn...  13.9 us
    dot_general x1, matrix products, per_device(): logits = jnp.dot(rows_piece, head, preferred_element_type=jnp.float32)  5.85 us

profile of v8, /device:TPU:1, one launch (start us, length us, event | category | flops | bytes accessed | tf_op | source)
XLA Modules:
  0.0 72.7 jit_solution(1151974944111022602)
XLA Ops:
  0.6 0.0 copy-start
  0.6 1.2 %copy-done = bf16[1,1024,512]{2,1,0:T(8,128)(2,1)S(1)} copy-done((bf16[1,1024,512]{2,1,0:T(8,128)(2,1)S(1)}, bf16[1,1024,512]{2,1,0:T(8,128)(2,1)}, u32[]{:S(2)}) %copy-start) | copy-done | bytes 1048600
  1.9 0.7 compare_bitcast_fusion
  2.5 0.1 copy.18
  2.6 0.1 reduce-window.8
  2.7 0.1 add_reduce_fusion
  2.8 0.1 select_reduce_fusion.3
  2.9 1.3 %gather_fusion = s32[16]{0:T(128)S(1)} fusion(s32[32]{0:T(128)} %bitcast.45, s32[1024]{0:T(1024)S(1)} %pad_clamp_fusion.1), kind=kCustom, calls=%fused_computation | custom fusion | bytes 192 | tf_op jit(solution)/shard_map/gather | solution.py:298
  4.9 0.6 gather_fusion.1
  5.5 0.7 broadcast_select_fusion.rows_ref
  6.2 1.3 %gather_fusion.2 = s32[16]{0:T(128)S(1)} fusion(s32[32]{0:T(128)} %bitcast.46, s32[1024]{0:T(1024)S(1)} %pad_clamp_fusion.1), kind=kCustom, calls=%fused_computation.2 | custom fusion | bytes 192 | tf_op jit(solution)/shard_map/gather | solution.py:301
  7.5 0.7 copy.19.target_ref
  8.2 40.8 %shard_map.86 = bf16[32,16,4224]{2,1,0:T(8,128)(2,1)} custom-call(bf16[16,512]{1,0:T(8,128)(2,1)} %broadcast_select_fusion.rows_ref, f32[1,4096]{1,0:T(1,128)} %bitcast.53, s32[16,1]{1,0:T(8,128)} %copy.19.target_ref), custom_call_target="tpu_custom_call" | custom-call | tf_op jit(solution)/shard_map/pallas_call | solution.py:267
  49.1 5.9 %fusion.9 = (f32[512]{0:T(512)S(1)}, f32[512,512]{0,1:T(8,128)S(1)}) fusion(bf16[4096,512]{1,0:T(8,128)(2,1)} %param.9, bf16[512,4224]{1,0:T(8,128)(2,1)} %bitcast.47), kind=kOutput, calls=%fused_computation.47 | convolution fusion | flops 2147745280 | bytes 9439232 | tf_op jit(solution)/shard_map/dot_general | solution.py:311
  54.9 0.9 %slice.27 = bf16[512,3]{1,0:T(8,128)(2,1)S(1)} slice(bf16[512,4224]{1,0:T(8,128)(2,1)} %bitcast.48), slice={[0:512], [4096:4099]} | slice | bytes 6144 | tf_op jit(solution)/shard_map/slice | solution.py:309
  55.8 0.1 copy.25
  56.0 0.3 fusion.2
  56.3 0.1 stack.18
  56.4 0.1 stack.17
  56.5 0.1 stack.16
  56.6 0.1 stack.15
  56.6 0.7 maximum_bitcast_fusion.part_ref
  57.3 13.9 %shard_map.87 = f32[4,16]{1,0:T(4,128)} custom-call(f32[32,4,16]{2,1,0:T(4,128)} %maximum_bitcast_fusion.part_ref), custom_call_target="tpu_custom_call" | custom-call | tf_op jit(solution)/shard_map/pallas_call | solution.py:108
  71.3 0.8 %subtract_bitcast_fusion.1 = (f32[16]{0:T(128)S(1)}, f32[16]{0:T(128)S(1)}) fusion(f32[4,16]{1,0:T(4,128)} %shard_map.87), kind=kLoop, calls=%fused_computation.45 | loop fusion | flops 64 | bytes 384 | tf_op jit(solution)/shard_map/sub | solution.py:322
  72.1 0.6 select_reduce_fusion.1
  (7 shorter events, 0.1 us)
Async XLA Ops:
  0.6 1.2 %copy-start = (bf16[1,1024,512]{2,1,0:T(8,128)(2,1)S(1)}, bf16[1,1024,512]{2,1,0:T(8,128)(2,1)}, u32[]{:S(2)}) copy-start(bf16[1,1024,512]{2,1,0:T(8,128)(2,1)} %param.7) | copy-start | bytes 3145732

commit v9 on v8

--- a/solution.py
+++ b/solution.py
@@ -120,7 +120,7 @@
             pltpu.SemaphoreType.DMA((n_t,)),
             pltpu.SemaphoreType.DMA((2,)),
         ],
-        compiler_params=pltpu.CompilerParams(collective_id=0, has_side_effects=True),
+        compiler_params=pltpu.CompilerParams(collective_id=0, has_side_effects=True, vmem_limit_bytes=16 * 1024 * 1024),
     )(parts)
 
 
@@ -278,7 +278,7 @@
             pltpu.SemaphoreType.DMA((n_dp,)),
             pltpu.SemaphoreType.DMA((2,)),
         ],
-        compiler_params=pltpu.CompilerParams(collective_id=2, has_side_effects=True),
+        compiler_params=pltpu.CompilerParams(collective_id=2, has_side_effects=True, vmem_limit_bytes=16 * 1024 * 1024),
     )(rows, gain.reshape(1, n_t * width), target.reshape(k, 1))
 
 

time: 73 us -> 64.9 us (0.89)
  matrix products: 5.85 us -> 2.38 us
  other arithmetic: 4.17 us -> 2.14 us
  Pallas kernels: 54.7 us -> 53 us
  local copies, waits for them, and re-layouts: 6.54 us -> 5.77 us
    dot_general x1, matrix products: 5.85 us -> 2.38 us  [per_device(): logits = jnp.dot(rows_piece, head, preferred_element_type=jnp.float32)]
    pallas_call x1, Pallas kernels: 40.8 us -> 39 us  [gather_rows(): pl.pallas_call(rows_kernel, out_shape=jax.ShapeDtypeStruct((n_dp,) + shap...]
    slice x1, local copies, waits for them, and re-layouts: 0.91 us -> 0.01 us  [per_device(): got_digits = gathered[:, width:width + 3].astype(jnp.int32)]
    sub x1, other arithmetic: 0.81 us -> 0.01 us  [per_device(): score = chosen - lse]
    unnamed x3 -> x7, local copies, waits for them, and re-layouts: 1.33 us -> 2.05 us
where the time goes in v9:
time: 64.9 us; the launch traced here: 64.7 us
  Pallas kernels  53 us (82%)
  local copies, waits for them, and re-layouts  5.77 us (9%)
  matrix products  2.38 us (4%)
  other arithmetic  2.14 us (3%)
  between operations  1.4 us (2%)
    pallas_call x1, Pallas kernels, gather_rows(): pl.pallas_call(rows_kernel, out_shape=jax.ShapeDtypeStruct((n_dp,) + shap...  39 us
    pallas_call x1, Pallas kernels, exchange_stats(): pl.pallas_call(stats_kernel, out_shape=jax.ShapeDtypeStruct((four, k), jn...  14 us
    dot_general x1, matrix products, per_device(): logits = jnp.dot(rows_piece, head, preferred_element_type=jnp.float32)  2.38 us
    unnamed x7, local copies, waits for them, and re-layouts  2.05 us
    gather x1, local copies, waits for them, and re-layouts, per_device(): position = lengths[seq_of] - 1 - offsets.reshape(slots)[idx]  1.32 us
    gather x1, local copies, waits for them, and re-layouts, per_device(): flat_target = targets.reshape(slots)[idx]  1.31 us

profile of v9, /device:TPU:1, one launch (start us, length us, event | category | flops | bytes accessed | tf_op | source)
XLA Modules:
  0.0 64.7 jit_solution(15659289843751645719)
XLA Ops:
  0.6 0.0 copy-start
  0.6 1.2 %copy-done = bf16[1,1024,512]{2,1,0:T(8,128)(2,1)S(1)} copy-done((bf16[1,1024,512]{2,1,0:T(8,128)(2,1)S(1)}, bf16[1,1024,512]{2,1,0:T(8,128)(2,1)}, u32[]{:S(2)}) %copy-start) | copy-done | bytes 1048600
  1.9 0.7 %compare_bitcast_fusion = (pred[32]{0:T(512)(128)(4,1)S(1)}, s32[32,1]{0,1:T(1,128)S(1)}) fusion(s32[1,32]{1,0:T(1,128)} %param.13), kind=kLoop, calls=%fused_computation.38 | loop fusion | flops 64 | bytes 288 | tf_op jit(solution)/shard_map/and | solution.py:295
  2.5 0.1 copy.18
  2.6 0.1 reduce-window.8
  2.7 0.1 add_reduce_fusion
  2.8 0.1 select_reduce_fusion.3
  2.9 1.3 %gather_fusion = s32[16]{0:T(128)S(1)} fusion(s32[32]{0:T(128)} %bitcast.48, s32[1024]{0:T(1024)S(1)} %pad_clamp_fusion.1), kind=kCustom, calls=%fused_computation | custom fusion | bytes 192 | tf_op jit(solution)/shard_map/gather | solution.py:298
  4.9 0.6 gather_fusion.1
  5.5 0.1 broadcast_select_fusion.rows_ref
  5.6 1.3 %gather_fusion.2 = s32[16]{0:T(128)S(1)} fusion(s32[32]{0:T(128)} %bitcast.49, s32[1024]{0:T(1024)S(1)} %pad_clamp_fusion.1), kind=kCustom, calls=%fused_computation.2 | custom fusion | bytes 192 | tf_op jit(solution)/shard_map/gather | solution.py:301
  6.9 0.1 copy.19.target_ref
  7.0 0.0 copy-start.1
  7.0 0.7 %copy-done.1 = f32[4096]{0:T(1024)S(1)} copy-done((f32[4096]{0:T(1024)S(1)}, f32[4096]{0:T(1024)}, u32[]{:S(2)}) %copy-start.1) | copy-done | bytes 16408
  7.8 0.0 copy-start.2
  7.8 39.0 %shard_map.86 = bf16[32,16,4224]{2,1,0:T(8,128)(2,1)S(1)} custom-call(bf16[16,512]{1,0:T(8,128)(2,1)S(1)} %broadcast_select_fusion.rows_ref, f32[1,4096]{1,0:T(1,128)S(1)} %bitcast.47, s32[16,1]{1,0:T(8,128)S(1)} %copy.19.target_ref), custom_call_target="tpu_custom_call" | custom-call | tf_op jit(solution)/shard_map/pallas_call | solution.py:267
  46.8 0.0 copy-done.2
  46.8 2.4 %fusion.9 = (f32[512]{0:T(512)S(1)}, f32[512,512]{0,1:T(8,128)S(1)}) fusion(bf16[4096,512]{1,0:T(8,128)(2,1)S(1)} %copy-done.2, bf16[512,4224]{1,0:T(8,128)(2,1)S(1)} %bitcast.45), kind=kOutput, calls=%fused_computation.47 | convolution fusion | flops 2147745280 | bytes 9439232 | tf_op jit(solution)/shard_map/dot_general | solution.py:311
  49.2 0.1 copy.25
  49.3 0.3 fusion.2
  49.7 0.1 stack.18
  49.8 0.1 stack.17
  49.8 0.1 stack.16
  49.9 0.1 stack.15
  50.0 0.1 maximum_bitcast_fusion.part_ref
  50.1 14.0 %shard_map.87 = f32[4,16]{1,0:T(4,128)S(1)} custom-call(f32[32,4,16]{2,1,0:T(4,128)S(1)} %maximum_bitcast_fusion.part_ref), custom_call_target="tpu_custom_call" | custom-call | tf_op jit(solution)/shard_map/pallas_call | solution.py:108
  64.1 0.6 select_reduce_fusion.1
  (9 shorter events, 0.1 us)
Async XLA Ops:
  0.6 1.2 %copy-start = (bf16[1,1024,512]{2,1,0:T(8,128)(2,1)S(1)}, bf16[1,1024,512]{2,1,0:T(8,128)(2,1)}, u32[]{:S(2)}) copy-start(bf16[1,1024,512]{2,1,0:T(8,128)(2,1)} %param.7) | copy-start | bytes 3145732
  7.0 0.7 %copy-start.1 = (f32[4096]{0:T(1024)S(1)}, f32[4096]{0:T(1024)}, u32[]{:S(2)}) copy-start(f32[4096]{0:T(1024)} %param.8) | copy-start | bytes 49156
  7.8 39.0 %copy-start.2 = (bf16[4096,512]{1,0:T(8,128)(2,1)S(1)}, bf16[4096,512]{1,0:T(8,128)(2,1)}, u32[]{:S(2)}) copy-start(bf16[4096,512]{1,0:T(8,128)(2,1)} %param.9) | copy-start | bytes 12582916

commit v10 on v9

--- a/solution.py
+++ b/solution.py
@@ -290,15 +290,17 @@
     n_t = lax.axis_size("tensor")
     k = min(LIVE, slots)
 
-    live = mask.reshape(slots) != 0
-    rank = jnp.cumsum(live.astype(jnp.int32)) - 1
-    sel = live[None, :] & (rank[None, :] == jnp.arange(k, dtype=jnp.int32)[:, None])
-    idx = jnp.sum(jnp.where(sel, jnp.arange(slots, dtype=jnp.int32)[None, :], 0), axis=1)
-    seq_of = idx // slot_count
-    position = lengths[seq_of] - 1 - offsets.reshape(slots)[idx]
+    live = (mask.reshape(slots) != 0).astype(jnp.int32)
+    slot_ids = jnp.arange(slots, dtype=jnp.int32)
+    rank = jnp.sum(jnp.where(slot_ids[:, None] >= slot_ids[None, :], live[None, :], 0), axis=1) - 1
+    sel = (live[None, :] != 0) & (rank[None, :] == jnp.arange(k, dtype=jnp.int32)[:, None])
+    seq_of = jnp.sum(jnp.where(sel, (slot_ids // slot_count)[None, :], 0), axis=1)
+    offset_of = jnp.sum(jnp.where(sel, offsets.reshape(1, slots), 0), axis=1)
+    flat_target = jnp.sum(jnp.where(sel, targets.reshape(1, slots), 0), axis=1)
+    length_of = jnp.sum(jnp.where(seq_of[:, None] == jnp.arange(seq_count)[None, :], lengths[None, :], 0), axis=1)
+    position = length_of - 1 - offset_of
     flat_hidden = hidden.reshape(seq_count * maxlen, hidden.shape[2])
     picked = jnp.take(flat_hidden, seq_of * maxlen + position, axis=0)
-    flat_target = targets.reshape(slots)[idx]
 
     vocab_width = head.shape[1]
     vocab_start = (lax.axis_index("dp") * n_t + lax.axis_index("tensor")) * vocab_width

time: 64.9 us -> 62.8 us (0.968)
  local copies, waits for them, and re-layouts: 5.77 us -> 3.04 us
    gather x2 -> x0, local copies, waits for them, and re-layouts: 2.63 us -> none  [the longest x1 1.32 us: per_device(): position = lengths[seq_of] - 1 - offsets.reshape(slots)[idx]]
    reduce_sum x1 -> x2, other arithmetic: 0.12 us -> 0.94 us  [the longest x1 0.82 us: per_device(): flat_target = jnp.sum(jnp.where(sel, targets.reshape(1, slots), 0), axis=1)]
where the time goes in v10:
time: 62.8 us; the launch traced here: 62.6 us
  Pallas kernels  53 us (84%)
  local copies, waits for them, and re-layouts  3.04 us (5%)
  other arithmetic  2.77 us (4%)
  matrix products  2.38 us (4%)
  between operations  1.4 us (2%)
    pallas_call x1, Pallas kernels, gather_rows(): pl.pallas_call(rows_kernel, out_shape=jax.ShapeDtypeStruct((n_dp,) + shap...  39 us
    pallas_call x1, Pallas kernels, exchange_stats(): pl.pallas_call(stats_kernel, out_shape=jax.ShapeDtypeStruct((four, k), jn...  14 us
    dot_general x1, matrix products, per_device(): logits = jnp.dot(rows_piece, head, preferred_element_type=jnp.float32)  2.38 us
    unnamed x7, local copies, waits for them, and re-layouts  2.05 us

profile of v10, /device:TPU:1, one launch (start us, length us, event | category | flops | bytes accessed | tf_op | source)
XLA Modules:
  0.0 62.6 jit_solution(18398986885410888023)
XLA Ops:
  0.6 0.0 copy-start
  0.6 1.2 %copy-done = bf16[1,1024,512]{2,1,0:T(8,128)(2,1)S(1)} copy-done((bf16[1,1024,512]{2,1,0:T(8,128)(2,1)S(1)}, bf16[1,1024,512]{2,1,0:T(8,128)(2,1)}, u32[]{:S(2)}) %copy-start) | copy-done | bytes 1048600
  1.9 0.7 %compare_bitcast_fusion = (pred[32]{0:T(512)(128)(4,1)S(1)}, s32[32]{0:T(128)S(1)}) fusion(s32[1,32]{1,0:T(1,128)} %param.13), kind=kLoop, calls=%fused_computation.30 | loop fusion | flops 96 | bytes 288 | tf_op jit(solution)/shard_map/and | solution.py:296
  2.5 0.1 select_reduce_fusion.1
  2.6 0.8 %select_reduce_fusion.4 = (s32[16]{0:T(128)S(1)}, s32[16]{0:T(128)S(1)}, s32[16]{0:T(128)S(1)}) fusion(s32[32]{0:T(128)} %bitcast.42, s32[32]{0:T(128)S(1)} %get-tuple-element.19, pred[32]{0:T(512)(128)(4,1)S(1)} %get-tuple-element.14, s32[32]{0:T(128)} %bitcast.43, s32[32]{0:T(128)S(1)} %get-tuple-element.18), kind=kLoop, calls=%fused_computation.14 | loop fusion | flops 4048 | bytes 736 | tf_op jit(solution)/shard_map/reduce_sum | solution.py:299
  4.2 0.6 gather_fusion
  4.8 0.1 broadcast_select_fusion.rows_ref
  4.8 0.1 copy.16.target_ref
  4.9 0.0 copy-start.1
  4.9 0.7 %copy-done.1 = f32[4096]{0:T(1024)S(1)} copy-done((f32[4096]{0:T(1024)S(1)}, f32[4096]{0:T(1024)}, u32[]{:S(2)}) %copy-start.1) | copy-done | bytes 16408
  5.6 0.0 copy-start.2
  5.6 39.0 %shard_map.86 = bf16[32,16,4224]{2,1,0:T(8,128)(2,1)S(1)} custom-call(bf16[16,512]{1,0:T(8,128)(2,1)S(1)} %broadcast_select_fusion.rows_ref, f32[1,4096]{1,0:T(1,128)S(1)} %bitcast.33, s32[16,1]{1,0:T(8,128)S(1)} %copy.16.target_ref), custom_call_target="tpu_custom_call" | custom-call | tf_op jit(solution)/shard_map/pallas_call | solution.py:267
  44.7 0.0 copy-done.2
  44.7 2.4 %fusion.12 = (f32[512]{0:T(512)S(1)}, f32[512,512]{0,1:T(8,128)S(1)}) fusion(bf16[4096,512]{1,0:T(8,128)(2,1)S(1)} %copy-done.2, bf16[512,4224]{1,0:T(8,128)(2,1)S(1)} %bitcast.31), kind=kOutput, calls=%fused_computation.44 | convolution fusion | flops 2147745280 | bytes 9439232 | tf_op jit(solution)/shard_map/dot_general | solution.py:313
  47.1 0.1 copy.22
  47.2 0.3 fusion.2
  47.6 0.1 stack.18
  47.6 0.1 stack.17
  47.7 0.1 stack.16
  47.8 0.1 stack.15
  47.9 0.1 maximum_bitcast_fusion.part_ref
  48.0 14.0 %shard_map.87 = f32[4,16]{1,0:T(4,128)S(1)} custom-call(f32[32,4,16]{2,1,0:T(4,128)S(1)} %maximum_bitcast_fusion.part_ref), custom_call_target="tpu_custom_call" | custom-call | tf_op jit(solution)/shard_map/pallas_call | solution.py:108
  62.0 0.6 select_reduce_fusion.2
  (8 shorter events, 0.1 us)
Async XLA Ops:
  0.6 1.2 %copy-start = (bf16[1,1024,512]{2,1,0:T(8,128)(2,1)S(1)}, bf16[1,1024,512]{2,1,0:T(8,128)(2,1)}, u32[]{:S(2)}) copy-start(bf16[1,1024,512]{2,1,0:T(8,128)(2,1)} %param.7) | copy-start | bytes 3145732
  4.9 0.7 %copy-start.1 = (f32[4096]{0:T(1024)S(1)}, f32[4096]{0:T(1024)}, u32[]{:S(2)}) copy-start(f32[4096]{0:T(1024)} %param.8) | copy-start | bytes 49156
  5.6 39.0 %copy-start.2 = (bf16[4096,512]{1,0:T(8,128)(2,1)S(1)}, bf16[4096,512]{1,0:T(8,128)(2,1)}, u32[]{:S(2)}) copy-start(bf16[4096,512]{1,0:T(8,128)(2,1)} %param.9) | copy-start | bytes 12582916

commit v11 on v10

--- a/solution.py
+++ b/solution.py
@@ -205,57 +205,69 @@
     block_ref[:, pl.ds(n_t * width, 128)] = tail.astype(jnp.float32).astype(block_ref.dtype)
 
     sends = []
-
-    def put(src_slot, dst_slot, target):
+    cols = block_ref.shape[1]
+    split = (cols // 256) * 128
+    halves = ((0, split), (split, cols - split))
+
+    def put(src_slot, dst_slot, target, h):
+        c0, cw = halves[h]
         src = block_ref if src_slot is None else out_ref.at[src_slot]
         copy = pltpu.make_async_remote_copy(
-            src_ref=src, dst_ref=out_ref.at[dst_slot], send_sem=send.at[len(sends)],
-            recv_sem=recv.at[dst_slot], device_id=target, device_id_type=MESH)
+            src_ref=src.at[:, pl.ds(c0, cw)], dst_ref=out_ref.at[dst_slot, :, pl.ds(c0, cw)],
+            send_sem=send.at[len(sends)], recv_sem=recv.at[dst_slot, h], device_id=target,
+            device_id_type=MESH)
         copy.start()
         sends.append(copy)
 
-    def arrive(dst_slot):
+    def arrive(dst_slot, h):
+        c0, cw = halves[h]
         pltpu.make_async_remote_copy(
-            src_ref=block_ref, dst_ref=out_ref.at[dst_slot], send_sem=send.at[0],
-            recv_sem=recv.at[dst_slot], device_id=sib_dev, device_id_type=MESH).wait_recv()
+            src_ref=block_ref.at[:, pl.ds(c0, cw)], dst_ref=out_ref.at[dst_slot, :, pl.ds(c0, cw)],
+            send_sem=send.at[0], recv_sem=recv.at[dst_slot, h], device_id=sib_dev,
+            device_id_type=MESH).wait_recv()
 
     own = pltpu.make_async_copy(block_ref, out_ref.at[me], local.at[0])
     own.start()
-    for target in (plus_a, minus_a, plus_b, minus_b, sib_dev):
-        put(None, me, target)
+    for h in (0, 1):
+        for target in (plus_a, minus_a, plus_b, minus_b, sib_dev):
+            put(None, me, target, h)
 
     left, right, far = slot(ua - 1, ub, core), slot(ua + 1, ub, core), slot(ua + 2, ub, core)
-    arrive(left)
-    for target in (plus_b, minus_b, sib_dev):
-        put(left, left, target)
-    arrive(right)
-    for target in (plus_b, minus_b, sib_dev):
-        put(right, right, target)
     pick = 1 - (ua + 3 + core) % 2
     fwd = pick * left + (1 - pick) * right
     fwd_dev = (pick * plus_a[0] + (1 - pick) * minus_a[0], mt)
-    put(fwd, fwd, fwd_dev)
-    arrive(far)
-    for target in (plus_b, minus_b, sib_dev):
-        put(far, far, target)
+    for h in (0, 1):
+        arrive(left, h)
+        arrive(right, h)
+        put(fwd, fwd, fwd_dev, h)
+        for src in (left, right):
+            for target in (plus_b, minus_b, sib_dev):
+                put(src, src, target, h)
+    for h in (0, 1):
+        arrive(far, h)
+        for target in (plus_b, minus_b, sib_dev):
+            put(far, far, target, h)
 
     pick_b = 1 - (ub + 3 + core) % 2
     for d in (0, -1, 1, 2):
         lo, hi = slot(ua + d, ub - 1, core), slot(ua + d, ub + 1, core)
-        arrive(lo)
-        put(lo, lo, sib_dev)
-        arrive(hi)
-        put(hi, hi, sib_dev)
         fwd = pick_b * lo + (1 - pick_b) * hi
         fwd_dev = (pick_b * plus_b[0] + (1 - pick_b) * minus_b[0], mt)
-        put(fwd, fwd, fwd_dev)
+        for h in (0, 1):
+            arrive(lo, h)
+            arrive(hi, h)
+            put(fwd, fwd, fwd_dev, h)
+            put(lo, lo, sib_dev, h)
+            put(hi, hi, sib_dev, h)
     for d in (0, -1, 1, 2):
         far_b = slot(ua + d, ub + 2, core)
-        arrive(far_b)
-        put(far_b, far_b, sib_dev)
+        for h in (0, 1):
+            arrive(far_b, h)
+            put(far_b, far_b, sib_dev, h)
 
     for c in range(n_chip):
-        arrive(c * 2 + 1 - core)
+        for h in (0, 1):
+            arrive(c * 2 + 1 - core, h)
     for copy in sends:
         copy.wait_send()
     own.wait()
@@ -274,8 +286,8 @@
             pltpu.VMEM(shape, rows.dtype),
             pltpu.SemaphoreType.DMA((n_t,)),
             pltpu.SemaphoreType.DMA((n_t,)),
-            pltpu.SemaphoreType.DMA((n_dp,)),
-            pltpu.SemaphoreType.DMA((n_dp,)),
+            pltpu.SemaphoreType.DMA((2 * n_dp,)),
+            pltpu.SemaphoreType.DMA((n_dp, 2)),
             pltpu.SemaphoreType.DMA((2,)),
         ],
         compiler_params=pltpu.CompilerParams(collective_id=2, has_side_effects=True, vmem_limit_bytes=16 * 1024 * 1024),

time: 62.8 us -> 61.6 us (0.981)
  Pallas kernels: 53 us -> 51.8 us
    pallas_call x1, Pallas kernels: 14 us -> 13.3 us  [exchange_stats(): pl.pallas_call(stats_kernel, out_shape=jax.ShapeDtypeStruct((four, k), jn...]
where the time goes in v11:
time: 61.6 us; the launch traced here: 61.4 us
  Pallas kernels  51.8 us (84%)
  local copies, waits for them, and re-layouts  3.04 us (5%)
  other arithmetic  2.77 us (4%)
  matrix products  2.38 us (4%)
  between operations  1.4 us (2%)
    pallas_call x1, Pallas kernels, gather_rows(): pl.pallas_call(rows_kernel, out_shape=jax.ShapeDtypeStruct((n_dp,) + shap...  38.5 us
    pallas_call x1, Pallas kernels, exchange_stats(): pl.pallas_call(stats_kernel, out_shape=jax.ShapeDtypeStruct((four, k), jn...  13.3 us
    dot_general x1, matrix products, per_device(): logits = jnp.dot(rows_piece, head, preferred_element_type=jnp.float32)  2.38 us
    unnamed x7, local copies, waits for them, and re-layouts  2.05 us

profile of v11, /device:TPU:1, one launch (start us, length us, event | category | flops | bytes accessed | tf_op | source)
XLA Modules:
  0.0 61.4 jit_solution(8039435903419669131)
XLA Ops:
  0.6 0.0 copy-start
  0.6 1.2 %copy-done = bf16[1,1024,512]{2,1,0:T(8,128)(2,1)S(1)} copy-done((bf16[1,1024,512]{2,1,0:T(8,128)(2,1)S(1)}, bf16[1,1024,512]{2,1,0:T(8,128)(2,1)}, u32[]{:S(2)}) %copy-start) | copy-done | bytes 1048600
  1.9 0.7 %compare_bitcast_fusion = (pred[32]{0:T(512)(128)(4,1)S(1)}, s32[32]{0:T(128)S(1)}) fusion(s32[1,32]{1,0:T(1,128)} %param.13), kind=kLoop, calls=%fused_computation.30 | loop fusion | flops 96 | bytes 288 | tf_op jit(solution)/shard_map/and | solution.py:308
  2.5 0.1 select_reduce_fusion.1
  2.6 0.8 %select_reduce_fusion.4 = (s32[16]{0:T(128)S(1)}, s32[16]{0:T(128)S(1)}, s32[16]{0:T(128)S(1)}) fusion(s32[32]{0:T(128)} %bitcast.42, s32[32]{0:T(128)S(1)} %get-tuple-element.19, pred[32]{0:T(512)(128)(4,1)S(1)} %get-tuple-element.14, s32[32]{0:T(128)} %bitcast.43, s32[32]{0:T(128)S(1)} %get-tuple-element.18), kind=kLoop, calls=%fused_computation.14 | loop fusion | flops 4048 | bytes 736 | tf_op jit(solution)/shard_map/reduce_sum | solution.py:311
  4.2 0.6 gather_fusion
  4.8 0.1 broadcast_select_fusion.rows_ref
  4.8 0.1 copy.16.target_ref
  4.9 0.0 copy-start.1
  4.9 0.7 %copy-done.1 = f32[4096]{0:T(1024)S(1)} copy-done((f32[4096]{0:T(1024)S(1)}, f32[4096]{0:T(1024)}, u32[]{:S(2)}) %copy-start.1) | copy-done | bytes 16408
  5.6 0.0 copy-start.2
  5.6 38.5 %shard_map.86 = bf16[32,16,4224]{2,1,0:T(8,128)(2,1)S(1)} custom-call(bf16[16,512]{1,0:T(8,128)(2,1)S(1)} %broadcast_select_fusion.rows_ref, f32[1,4096]{1,0:T(1,128)S(1)} %bitcast.33, s32[16,1]{1,0:T(8,128)S(1)} %copy.16.target_ref), custom_call_target="tpu_custom_call" | custom-call | tf_op jit(solution)/shard_map/pallas_call | solution.py:279
  44.2 0.0 copy-done.2
  44.2 2.4 %fusion.12 = (f32[512]{0:T(512)S(1)}, f32[512,512]{0,1:T(8,128)S(1)}) fusion(bf16[4096,512]{1,0:T(8,128)(2,1)S(1)} %copy-done.2, bf16[512,4224]{1,0:T(8,128)(2,1)S(1)} %bitcast.31), kind=kOutput, calls=%fused_computation.44 | convolution fusion | flops 2147745280 | bytes 9439232 | tf_op jit(solution)/shard_map/dot_general | solution.py:325
  46.6 0.1 copy.22
  46.7 0.3 fusion.2
  47.1 0.1 stack.18
  47.1 0.1 stack.17
  47.2 0.1 stack.16
  47.3 0.1 stack.15
  47.4 0.1 maximum_bitcast_fusion.part_ref
  47.5 13.3 %shard_map.87 = f32[4,16]{1,0:T(4,128)S(1)} custom-call(f32[32,4,16]{2,1,0:T(4,128)S(1)} %maximum_bitcast_fusion.part_ref), custom_call_target="tpu_custom_call" | custom-call | tf_op jit(solution)/shard_map/pallas_call | solution.py:108
  60.8 0.6 select_reduce_fusion.2
  (8 shorter events, 0.1 us)
Async XLA Ops:
  0.6 1.2 %copy-start = (bf16[1,1024,512]{2,1,0:T(8,128)(2,1)S(1)}, bf16[1,1024,512]{2,1,0:T(8,128)(2,1)}, u32[]{:S(2)}) copy-start(bf16[1,1024,512]{2,1,0:T(8,128)(2,1)} %param.7) | copy-start | bytes 3145732
  4.9 0.7 %copy-start.1 = (f32[4096]{0:T(1024)S(1)}, f32[4096]{0:T(1024)}, u32[]{:S(2)}) copy-start(f32[4096]{0:T(1024)} %param.8) | copy-start | bytes 49156
  5.6 38.5 %copy-start.2 = (bf16[4096,512]{1,0:T(8,128)(2,1)S(1)}, bf16[4096,512]{1,0:T(8,128)(2,1)}, u32[]{:S(2)}) copy-start(bf16[4096,512]{1,0:T(8,128)(2,1)} %param.9) | copy-start | bytes 12582916

commit v12 on v11

--- a/solution.py
+++ b/solution.py
@@ -13,20 +13,28 @@
 
 
 def merge(parts):
-    tops = parts[:, 0, :]
-    top = jnp.max(tops, axis=0, keepdims=True)
-    factor = jnp.exp(tops - top)
-    total = jnp.sum(parts[:, 1, :] * factor, axis=0, keepdims=True)
-    weighted = jnp.sum(parts[:, 2, :] * factor, axis=0, keepdims=True)
-    chosen = jnp.sum(parts[:, 3, :], axis=0, keepdims=True)
-    return jnp.concatenate([top, total, weighted, chosen], axis=0)
-
-
-def stats_kernel(part_ref, out_ref, got1, sent, got2, send1, recv1, send2, recv2, local):
-    n_dp = part_ref.shape[0]
+    tops = parts[:, :, 0:1]
+    top = jnp.max(tops, axis=0)
+    factor = jnp.exp(tops - top[None])
+    total = jnp.sum(parts[:, :, 1:2] * factor, axis=0)
+    weighted = jnp.sum(parts[:, :, 2:3] * factor, axis=0)
+    chosen = jnp.sum(parts[:, :, 3:4], axis=0)
+    return pack(top, total, weighted, chosen)
+
+
+def pack(top, total, weighted, chosen):
+    lane = lax.broadcasted_iota(jnp.int32, (top.shape[0], 128), 1)
+    return jnp.where(lane == 0, top, jnp.where(lane == 1, total, jnp.where(
+        lane == 2, weighted, jnp.where(lane == 3, chosen, 0.0))))
+
+
+def stats_kernel(rows_ref, head_ref, out_ref, parts, got1, sent, got2, send1, recv1, send2, recv2, local):
+    n_dp, k, _ = got1.shape
     n_t = got2.shape[0]
     me = lax.axis_index("dp")
     mt = lax.axis_index("tensor")
+    vocab = head_ref.shape[1]
+    width = head_ref.shape[0]
 
     barrier = pltpu.get_barrier_semaphore()
 
@@ -42,16 +50,38 @@
 
     lax.fori_loop(0, n_dp - 1, greet_dp, 0)
     lax.fori_loop(0, n_t - 1, greet_t, 0)
+
+    vocab_start = (me * n_t + mt) * vocab
+    chunk = 128
+
+    def local_stats(c, carry):
+        r0 = pl.multiple_of(c * chunk, chunk)
+        logits = jnp.dot(rows_ref[pl.ds(r0, chunk), pl.ds(0, width)], head_ref[...],
+                         preferred_element_type=jnp.float32)
+        top = jnp.max(logits, axis=1, keepdims=True)
+        expo = jnp.exp(logits - top)
+        total = jnp.sum(expo, axis=1, keepdims=True)
+        weighted = jnp.sum(expo * logits, axis=1, keepdims=True)
+        digits = rows_ref[pl.ds(r0, chunk), pl.ds(width, 128)].astype(jnp.float32)
+        lane = lax.broadcasted_iota(jnp.int32, digits.shape, 1)
+        place = jnp.where(lane == 0, 65536.0, jnp.where(lane == 1, 256.0, jnp.where(lane == 2, 1.0, 0.0)))
+        target = jnp.sum(digits * place, axis=1, keepdims=True).astype(jnp.int32)
+        column = lax.broadcasted_iota(jnp.int32, logits.shape, 1) + vocab_start
+        chosen = jnp.sum(jnp.where(column == target, logits, 0.0), axis=1, keepdims=True)
+        parts[pl.ds(r0, chunk), :] = pack(top, total, weighted, chosen)
+        return carry
+
+    lax.fori_loop(0, rows_ref.shape[0] // chunk, local_stats, 0)
     pl.semaphore_wait(barrier, n_dp - 1 + n_t - 1)
 
     def out1(p):
         return pltpu.make_async_remote_copy(
-            src_ref=part_ref.at[p], dst_ref=got1.at[me], send_sem=send1.at[p],
+            src_ref=parts.at[pl.ds(p * k, k)], dst_ref=got1.at[me], send_sem=send1.at[p],
             recv_sem=recv1.at[me], device_id=(p, mt), device_id_type=MESH)
 
     def in1(p):
         return pltpu.make_async_remote_copy(
-            src_ref=part_ref.at[p], dst_ref=got1.at[p], send_sem=send1.at[p],
+            src_ref=parts.at[pl.ds(p * k, k)], dst_ref=got1.at[p], send_sem=send1.at[p],
             recv_sem=recv1.at[p], device_id=(p, mt), device_id_type=MESH)
 
     def start1(i, carry):
@@ -59,7 +89,7 @@
         return carry
 
     lax.fori_loop(0, n_dp - 1, start1, 0)
-    own1 = pltpu.make_async_copy(part_ref.at[me], got1.at[me], local.at[0])
+    own1 = pltpu.make_async_copy(parts.at[pl.ds(me * k, k)], got1.at[me], local.at[0])
     own1.start()
 
     def finish1(i, carry):
@@ -103,25 +133,25 @@
     out_ref[...] = merge(got2[...])
 
 
-def exchange_stats(parts, n_t):
-    n_dp, four, k = parts.shape
+def exchange_stats(rows, head, n_dp, n_t, k):
     return pl.pallas_call(
         stats_kernel,
-        out_shape=jax.ShapeDtypeStruct((four, k), jnp.float32),
-        in_specs=[pl.BlockSpec(memory_space=pltpu.VMEM)],
+        out_shape=jax.ShapeDtypeStruct((k, 128), jnp.float32),
+        in_specs=[pl.BlockSpec(memory_space=pltpu.VMEM)] * 2,
         out_specs=pl.BlockSpec(memory_space=pltpu.VMEM),
         scratch_shapes=[
-            pltpu.VMEM((n_dp, four, k), jnp.float32),
-            pltpu.VMEM((four, k), jnp.float32),
-            pltpu.VMEM((n_t, four, k), jnp.float32),
+            pltpu.VMEM((n_dp * k, 128), jnp.float32),
+            pltpu.VMEM((n_dp, k, 128), jnp.float32),
+            pltpu.VMEM((k, 128), jnp.float32),
+            pltpu.VMEM((n_t, k, 128), jnp.float32),
             pltpu.SemaphoreType.DMA((n_dp,)),
             pltpu.SemaphoreType.DMA((n_dp,)),
             pltpu.SemaphoreType.DMA((n_t,)),
             pltpu.SemaphoreType.DMA((n_t,)),
             pltpu.SemaphoreType.DMA((2,)),
         ],
-        compiler_params=pltpu.CompilerParams(collective_id=0, has_side_effects=True, vmem_limit_bytes=16 * 1024 * 1024),
-    )(parts)
+        compiler_params=pltpu.CompilerParams(collective_id=0, has_side_effects=True, vmem_limit_bytes=32 * 1024 * 1024),
+    )(rows, head)
 
 
 def rows_kernel(rows_ref, gain_ref, target_ref, out_ref, got, block_ref, send_t, recv_t, send, recv, local):
@@ -314,24 +344,10 @@
     flat_hidden = hidden.reshape(seq_count * maxlen, hidden.shape[2])
     picked = jnp.take(flat_hidden, seq_of * maxlen + position, axis=0)
 
-    vocab_width = head.shape[1]
-    vocab_start = (lax.axis_index("dp") * n_t + lax.axis_index("tensor")) * vocab_width
-    columns = jnp.arange(vocab_width, dtype=jnp.int32)
     width = n_t * picked.shape[1]
     gathered = gather_rows(picked, gain, flat_target, n_dp, n_t).reshape(n_dp * k, width + 128)
-    rows_piece = gathered[:, :width]
-    got_digits = gathered[:, width : width + 3].astype(jnp.int32)
-    target_piece = got_digits[:, 0] * 65536 + got_digits[:, 1] * 256 + got_digits[:, 2]
-    logits = jnp.dot(rows_piece, head, preferred_element_type=jnp.float32)
-    top = jnp.max(logits, axis=-1)
-    expo = jnp.exp(logits - top[:, None])
-    total = jnp.sum(expo, axis=-1)
-    weighted = jnp.sum(expo * logits, axis=-1)
-    hit = columns[None, :] == (target_piece - vocab_start)[:, None]
-    chosen = jnp.sum(jnp.where(hit, logits, 0.0), axis=-1)
-
-    parts = jnp.stack([top, total, weighted, chosen]).reshape(4, n_dp, k).transpose(1, 0, 2)
-    top, total, weighted, chosen = exchange_stats(parts, n_t)
+    merged = exchange_stats(gathered, head, n_dp, n_t, k)
+    top, total, weighted, chosen = merged[:, 0], merged[:, 1], merged[:, 2], merged[:, 3]
     lse = top + jnp.log(total)
     score = chosen - lse
     spread = lse - weighted / total

time: 61.6 us -> 61.3 us (level)
  Pallas kernels: 51.8 us -> 55.2 us
  matrix products: 2.38 us -> 0 us
  local copies, waits for them, and re-layouts: 3.04 us -> 2.05 us
    pallas_call x1, Pallas kernels: 13.3 us -> 16.7 us  [exchange_stats(): pl.pallas_call(stats_kernel, out_shape=jax.ShapeDtypeStruct((k, 128), jnp...]
    dot_general x1 -> x0, matrix products: 2.38 us -> none  [per_device(): logits = jnp.dot(rows_piece, head, preferred_element_type=jnp.float32)]
    unnamed x7 -> x6, local copies, waits for them, and re-layouts: 2.05 us -> 1.38 us
where the time goes in v12:
time: 61.3 us; the launch traced here: 61.2 us
  Pallas kernels  55.2 us (90%)
  other arithmetic  2.5 us (4%)
  local copies, waits for them, and re-layouts  2.05 us (3%)
  between operations  1.43 us (2%)
    pallas_call x1, Pallas kernels, gather_rows(): pl.pallas_call(rows_kernel, out_shape=jax.ShapeDtypeStruct((n_dp,) + shap...  38.5 us
    pallas_call x1, Pallas kernels, exchange_stats(): pl.pallas_call(stats_kernel, out_shape=jax.ShapeDtypeStruct((k, 128), jnp...  16.7 us
    unnamed x6, local copies, waits for them, and re-layouts  1.38 us

profile of v12, /device:TPU:1, one launch (start us, length us, event | category | flops | bytes accessed | tf_op | source)
XLA Modules:
  0.0 61.2 jit_solution(5779841604682798404)
XLA Ops:
  0.6 0.0 copy-start
  1.4 0.5 copy-done
  1.9 0.7 %compare_bitcast_fusion = (pred[32]{0:T(512)(128)(4,1)S(1)}, s32[32]{0:T(128)S(1)}) fusion(s32[1,32]{1,0:T(1,128)} %param.13), kind=kLoop, calls=%fused_computation.20 | loop fusion | flops 96 | bytes 288 | tf_op jit(solution)/shard_map/and | solution.py:338
  2.5 0.1 select_reduce_fusion
  2.7 0.8 %select_reduce_fusion.3 = (s32[16]{0:T(128)S(1)}, s32[16]{0:T(128)S(1)}, s32[16]{0:T(128)S(1)}) fusion(s32[32]{0:T(128)} %bitcast.24, s32[32]{0:T(128)S(1)} %get-tuple-element.14, pred[32]{0:T(512)(128)(4,1)S(1)} %get-tuple-element.11, s32[32]{0:T(128)} %bitcast.25, s32[32]{0:T(128)S(1)} %get-tuple-element.13), kind=kLoop, calls=%fused_computation.9 | loop fusion | flops 4048 | bytes 736 | tf_op jit(solution)/shard_map/reduce_sum | solution.py:341
  3.5 0.1 copy.11.target_ref
  3.6 0.6 gather_fusion
  4.2 0.0 copy-start.1
  4.2 0.1 broadcast_select_fusion.rows_ref
  4.3 0.0 copy-start.2
  4.3 0.9 %copy-done.2 = f32[4096]{0:T(1024)S(1)} copy-done((f32[4096]{0:T(1024)S(1)}, f32[4096]{0:T(1024)}, u32[]{:S(2)}) %copy-start.2) | copy-done | bytes 16408
  5.2 38.5 %shard_map.86 = bf16[32,16,4224]{2,1,0:T(8,128)(2,1)S(1)} custom-call(bf16[16,512]{1,0:T(8,128)(2,1)S(1)} %broadcast_select_fusion.rows_ref, f32[1,4096]{1,0:T(1,128)S(1)} %bitcast.20, s32[16,1]{1,0:T(8,128)S(1)} %copy.11.target_ref), custom_call_target="tpu_custom_call" | custom-call | tf_op jit(solution)/shard_map/pallas_call | solution.py:309
  43.7 0.0 copy-done.1
  43.7 16.7 %shard_map.87 = f32[16,128]{1,0:T(8,128)S(1)} custom-call(bf16[512,4224]{1,0:T(8,128)(2,1)S(1)} %bitcast.19, bf16[4096,512]{1,0:T(8,128)(2,1)S(1)} %copy-done.1), custom_call_target="tpu_custom_call" | custom-call | tf_op jit(solution)/shard_map/pallas_call | solution.py:137
  60.4 0.2 subtract_reduce_fusion
  60.6 0.6 select_reduce_fusion.1
  (4 shorter events, 0.0 us)
Async XLA Ops:
  0.6 1.2 %copy-start = (bf16[1,1024,512]{2,1,0:T(8,128)(2,1)S(1)}, bf16[1,1024,512]{2,1,0:T(8,128)(2,1)}, u32[]{:S(2)}) copy-start(bf16[1,1024,512]{2,1,0:T(8,128)(2,1)} %param.7) | copy-start | bytes 3145732
  4.2 39.5 %copy-start.1 = (bf16[4096,512]{1,0:T(8,128)(2,1)S(1)}, bf16[4096,512]{1,0:T(8,128)(2,1)}, u32[]{:S(2)}) copy-start(bf16[4096,512]{1,0:T(8,128)(2,1)} %head_ref.1) | copy-start | bytes 12582916
  4.3 0.9 %copy-start.2 = (f32[4096]{0:T(1024)S(1)}, f32[4096]{0:T(1024)}, u32[]{:S(2)}) copy-start(f32[4096]{0:T(1024)} %param.8) | copy-start | bytes 49156

commit v13 on v11

--- a/solution.py
+++ b/solution.py
@@ -10,6 +10,7 @@
 MESH = pl.DeviceIdType.MESH
 LIVE = 16
 RING = 4
+PIECES = 4
 
 
 def merge(parts):
@@ -206,8 +207,9 @@
 
     sends = []
     cols = block_ref.shape[1]
-    split = (cols // 256) * 128
-    halves = ((0, split), (split, cols - split))
+    pieces = min(PIECES, cols // 128)
+    edges = [(cols // 128 * i // pieces) * 128 for i in range(pieces)] + [cols]
+    halves = tuple((edges[i], edges[i + 1] - edges[i]) for i in range(pieces))
 
     def put(src_slot, dst_slot, target, h):
         c0, cw = halves[h]
@@ -228,7 +230,7 @@
 
     own = pltpu.make_async_copy(block_ref, out_ref.at[me], local.at[0])
     own.start()
-    for h in (0, 1):
+    for h in range(pieces):
         for target in (plus_a, minus_a, plus_b, minus_b, sib_dev):
             put(None, me, target, h)
 
@@ -236,14 +238,14 @@
     pick = 1 - (ua + 3 + core) % 2
     fwd = pick * left + (1 - pick) * right
     fwd_dev = (pick * plus_a[0] + (1 - pick) * minus_a[0], mt)
-    for h in (0, 1):
+    for h in range(pieces):
         arrive(left, h)
         arrive(right, h)
         put(fwd, fwd, fwd_dev, h)
         for src in (left, right):
             for target in (plus_b, minus_b, sib_dev):
                 put(src, src, target, h)
-    for h in (0, 1):
+    for h in range(pieces):
         arrive(far, h)
         for target in (plus_b, minus_b, sib_dev):
             put(far, far, target, h)
@@ -253,7 +255,7 @@
         lo, hi = slot(ua + d, ub - 1, core), slot(ua + d, ub + 1, core)
         fwd = pick_b * lo + (1 - pick_b) * hi
         fwd_dev = (pick_b * plus_b[0] + (1 - pick_b) * minus_b[0], mt)
-        for h in (0, 1):
+        for h in range(pieces):
             arrive(lo, h)
             arrive(hi, h)
             put(fwd, fwd, fwd_dev, h)
@@ -261,12 +263,12 @@
             put(hi, hi, sib_dev, h)
     for d in (0, -1, 1, 2):
         far_b = slot(ua + d, ub + 2, core)
-        for h in (0, 1):
+        for h in range(pieces):
             arrive(far_b, h)
             put(far_b, far_b, sib_dev, h)
 
     for c in range(n_chip):
-        for h in (0, 1):
+        for h in range(pieces):
             arrive(c * 2 + 1 - core, h)
     for copy in sends:
         copy.wait_send()
@@ -286,8 +288,8 @@
             pltpu.VMEM(shape, rows.dtype),
             pltpu.SemaphoreType.DMA((n_t,)),
             pltpu.SemaphoreType.DMA((n_t,)),
-            pltpu.SemaphoreType.DMA((2 * n_dp,)),
-            pltpu.SemaphoreType.DMA((n_dp, 2)),
+            pltpu.SemaphoreType.DMA((PIECES * n_dp,)),
+            pltpu.SemaphoreType.DMA((n_dp, PIECES)),
             pltpu.SemaphoreType.DMA((2,)),
         ],
         compiler_params=pltpu.CompilerParams(collective_id=2, has_side_effects=True, vmem_limit_bytes=16 * 1024 * 1024),

time: 61.6 us -> 62 us (level)
  no operation moved by 1% of the time
where the time goes in v13:
time: 62 us; the launch traced here: 61.8 us
  Pallas kernels  52.2 us (84%)
  local copies, waits for them, and re-layouts  3.04 us (5%)
  other arithmetic  2.77 us (4%)
  matrix products  2.39 us (4%)
  between operations  1.4 us (2%)
    pallas_call x1, Pallas kernels, gather_rows(): pl.pallas_call(rows_kernel, out_shape=jax.ShapeDtypeStruct((n_dp,) + shap...  38.9 us
    pallas_call x1, Pallas kernels, exchange_stats(): pl.pallas_call(stats_kernel, out_shape=jax.ShapeDtypeStruct((four, k), jn...  13.3 us
    dot_general x1, matrix products, per_device(): logits = jnp.dot(rows_piece, head, preferred_element_type=jnp.float32)  2.39 us
    unnamed x7, local copies, waits for them, and re-layouts  2.05 us

profile of v13, /device:TPU:1, one launch (start us, length us, event | category | flops | bytes accessed | tf_op | source)
XLA Modules:
  0.0 61.8 jit_solution(731967657670962743)
XLA Ops:
  0.6 0.0 copy-start
  0.6 1.2 %copy-done = bf16[1,1024,512]{2,1,0:T(8,128)(2,1)S(1)} copy-done((bf16[1,1024,512]{2,1,0:T(8,128)(2,1)S(1)}, bf16[1,1024,512]{2,1,0:T(8,128)(2,1)}, u32[]{:S(2)}) %copy-start) | copy-done | bytes 1048600
  1.9 0.7 %compare_bitcast_fusion = (pred[32]{0:T(512)(128)(4,1)S(1)}, s32[32]{0:T(128)S(1)}) fusion(s32[1,32]{1,0:T(1,128)} %param.13), kind=kLoop, calls=%fused_computation.30 | loop fusion | flops 96 | bytes 288 | tf_op jit(solution)/shard_map/and | solution.py:310
  2.5 0.1 select_reduce_fusion.1
  2.6 0.8 %select_reduce_fusion.4 = (s32[16]{0:T(128)S(1)}, s32[16]{0:T(128)S(1)}, s32[16]{0:T(128)S(1)}) fusion(s32[32]{0:T(128)} %bitcast.42, s32[32]{0:T(128)S(1)} %get-tuple-element.19, pred[32]{0:T(512)(128)(4,1)S(1)} %get-tuple-element.14, s32[32]{0:T(128)} %bitcast.43, s32[32]{0:T(128)S(1)} %get-tuple-element.18), kind=kLoop, calls=%fused_computation.14 | loop fusion | flops 4048 | bytes 736 | tf_op jit(solution)/shard_map/reduce_sum | solution.py:313
  4.2 0.6 gather_fusion
  4.8 0.1 broadcast_select_fusion.rows_ref
  4.8 0.1 copy.16.target_ref
  4.9 0.0 copy-start.1
  4.9 0.7 %copy-done.1 = f32[4096]{0:T(1024)S(1)} copy-done((f32[4096]{0:T(1024)S(1)}, f32[4096]{0:T(1024)}, u32[]{:S(2)}) %copy-start.1) | copy-done | bytes 16408
  5.6 0.0 copy-start.2
  5.6 38.9 %shard_map.86 = bf16[32,16,4224]{2,1,0:T(8,128)(2,1)S(1)} custom-call(bf16[16,512]{1,0:T(8,128)(2,1)S(1)} %broadcast_select_fusion.rows_ref, f32[1,4096]{1,0:T(1,128)S(1)} %bitcast.33, s32[16,1]{1,0:T(8,128)S(1)} %copy.16.target_ref), custom_call_target="tpu_custom_call" | custom-call | tf_op jit(solution)/shard_map/pallas_call | solution.py:281
  44.5 0.0 copy-done.2
  44.5 2.4 %fusion.12 = (f32[512]{0:T(512)S(1)}, f32[512,512]{0,1:T(8,128)S(1)}) fusion(bf16[4096,512]{1,0:T(8,128)(2,1)S(1)} %copy-done.2, bf16[512,4224]{1,0:T(8,128)(2,1)S(1)} %bitcast.31), kind=kOutput, calls=%fused_computation.44 | convolution fusion | flops 2147745280 | bytes 9439232 | tf_op jit(solution)/shard_map/dot_general | solution.py:327
  46.9 0.1 copy.22
  47.1 0.3 fusion.2
  47.4 0.1 stack.18
  47.5 0.1 stack.17
  47.6 0.1 stack.16
  47.7 0.1 stack.15
  47.7 0.1 maximum_bitcast_fusion.part_ref
  47.8 13.3 %shard_map.87 = f32[4,16]{1,0:T(4,128)S(1)} custom-call(f32[32,4,16]{2,1,0:T(4,128)S(1)} %maximum_bitcast_fusion.part_ref), custom_call_target="tpu_custom_call" | custom-call | tf_op jit(solution)/shard_map/pallas_call | solution.py:109
  61.1 0.6 select_reduce_fusion.2
  (8 shorter events, 0.1 us)
Async XLA Ops:
  0.6 1.2 %copy-start = (bf16[1,1024,512]{2,1,0:T(8,128)(2,1)S(1)}, bf16[1,1024,512]{2,1,0:T(8,128)(2,1)}, u32[]{:S(2)}) copy-start(bf16[1,1024,512]{2,1,0:T(8,128)(2,1)} %param.7) | copy-start | bytes 3145732
  4.9 0.7 %copy-start.1 = (f32[4096]{0:T(1024)S(1)}, f32[4096]{0:T(1024)}, u32[]{:S(2)}) copy-start(f32[4096]{0:T(1024)} %param.8) | copy-start | bytes 49156
  5.6 38.9 %copy-start.2 = (bf16[4096,512]{1,0:T(8,128)(2,1)S(1)}, bf16[4096,512]{1,0:T(8,128)(2,1)}, u32[]{:S(2)}) copy-start(bf16[4096,512]{1,0:T(8,128)(2,1)} %param.9) | copy-start | bytes 12582916

commit v14 on v11

--- a/solution.py
+++ b/solution.py
@@ -236,10 +236,11 @@
     pick = 1 - (ua + 3 + core) % 2
     fwd = pick * left + (1 - pick) * right
     fwd_dev = (pick * plus_a[0] + (1 - pick) * minus_a[0], mt)
+    other = left + right - fwd
     for h in (0, 1):
-        arrive(left, h)
-        arrive(right, h)
+        arrive(fwd, h)
         put(fwd, fwd, fwd_dev, h)
+        arrive(other, h)
         for src in (left, right):
             for target in (plus_b, minus_b, sib_dev):
                 put(src, src, target, h)
@@ -253,10 +254,11 @@
         lo, hi = slot(ua + d, ub - 1, core), slot(ua + d, ub + 1, core)
         fwd = pick_b * lo + (1 - pick_b) * hi
         fwd_dev = (pick_b * plus_b[0] + (1 - pick_b) * minus_b[0], mt)
+        other = lo + hi - fwd
         for h in (0, 1):
-            arrive(lo, h)
-            arrive(hi, h)
+            arrive(fwd, h)
             put(fwd, fwd, fwd_dev, h)
+            arrive(other, h)
             put(lo, lo, sib_dev, h)
             put(hi, hi, sib_dev, h)
     for d in (0, -1, 1, 2):

time: 61.6 us -> 61.5 us (level)
  no operation moved by 1% of the time
where the time goes in v14:
time: 61.5 us; the launch traced here: 61.3 us
  Pallas kernels  51.7 us (84%)
  local copies, waits for them, and re-layouts  3.04 us (5%)
  other arithmetic  2.77 us (5%)
  matrix products  2.38 us (4%)
  between operations  1.4 us (2%)
    pallas_call x1, Pallas kernels, gather_rows(): pl.pallas_call(rows_kernel, out_shape=jax.ShapeDtypeStruct((n_dp,) + shap...  37.9 us
    pallas_call x1, Pallas kernels, exchange_stats(): pl.pallas_call(stats_kernel, out_shape=jax.ShapeDtypeStruct((four, k), jn...  13.8 us
    dot_general x1, matrix products, per_device(): logits = jnp.dot(rows_piece, head, preferred_element_type=jnp.float32)  2.38 us
    unnamed x7, local copies, waits for them, and re-layouts  2.05 us

profile of v14, /device:TPU:1, one launch (start us, length us, event | category | flops | bytes accessed | tf_op | source)
XLA Modules:
  0.0 61.3 jit_solution(16558978701451397007)
XLA Ops:
  0.6 0.0 copy-start
  0.6 1.2 %copy-done = bf16[1,1024,512]{2,1,0:T(8,128)(2,1)S(1)} copy-done((bf16[1,1024,512]{2,1,0:T(8,128)(2,1)S(1)}, bf16[1,1024,512]{2,1,0:T(8,128)(2,1)}, u32[]{:S(2)}) %copy-start) | copy-done | bytes 1048600
  1.9 0.7 %compare_bitcast_fusion = (pred[32]{0:T(512)(128)(4,1)S(1)}, s32[32]{0:T(128)S(1)}) fusion(s32[1,32]{1,0:T(1,128)} %param.13), kind=kLoop, calls=%fused_computation.30 | loop fusion | flops 96 | bytes 288 | tf_op jit(solution)/shard_map/and | solution.py:310
  2.5 0.1 select_reduce_fusion.1
  2.6 0.8 %select_reduce_fusion.4 = (s32[16]{0:T(128)S(1)}, s32[16]{0:T(128)S(1)}, s32[16]{0:T(128)S(1)}) fusion(s32[32]{0:T(128)} %bitcast.42, s32[32]{0:T(128)S(1)} %get-tuple-element.19, pred[32]{0:T(512)(128)(4,1)S(1)} %get-tuple-element.14, s32[32]{0:T(128)} %bitcast.43, s32[32]{0:T(128)S(1)} %get-tuple-element.18), kind=kLoop, calls=%fused_computation.14 | loop fusion | flops 4048 | bytes 736 | tf_op jit(solution)/shard_map/reduce_sum | solution.py:313
  4.2 0.6 gather_fusion
  4.8 0.1 broadcast_select_fusion.rows_ref
  4.8 0.1 copy.16.target_ref
  4.9 0.0 copy-start.1
  4.9 0.7 %copy-done.1 = f32[4096]{0:T(1024)S(1)} copy-done((f32[4096]{0:T(1024)S(1)}, f32[4096]{0:T(1024)}, u32[]{:S(2)}) %copy-start.1) | copy-done | bytes 16408
  5.6 0.0 copy-start.2
  5.6 37.9 %shard_map.86 = bf16[32,16,4224]{2,1,0:T(8,128)(2,1)S(1)} custom-call(bf16[16,512]{1,0:T(8,128)(2,1)S(1)} %broadcast_select_fusion.rows_ref, f32[1,4096]{1,0:T(1,128)S(1)} %bitcast.33, s32[16,1]{1,0:T(8,128)S(1)} %copy.16.target_ref), custom_call_target="tpu_custom_call" | custom-call | tf_op jit(solution)/shard_map/pallas_call | solution.py:281
  43.5 0.0 copy-done.2
  43.6 2.4 %fusion.12 = (f32[512]{0:T(512)S(1)}, f32[512,512]{0,1:T(8,128)S(1)}) fusion(bf16[4096,512]{1,0:T(8,128)(2,1)S(1)} %copy-done.2, bf16[512,4224]{1,0:T(8,128)(2,1)S(1)} %bitcast.31), kind=kOutput, calls=%fused_computation.44 | convolution fusion | flops 2147745280 | bytes 9439232 | tf_op jit(solution)/shard_map/dot_general | solution.py:327
  46.0 0.1 copy.22
  46.1 0.3 fusion.2
  46.4 0.1 stack.18
  46.5 0.1 stack.17
  46.6 0.1 stack.16
  46.7 0.1 stack.15
  46.8 0.1 maximum_bitcast_fusion.part_ref
  46.9 13.8 %shard_map.87 = f32[4,16]{1,0:T(4,128)S(1)} custom-call(f32[32,4,16]{2,1,0:T(4,128)S(1)} %maximum_bitcast_fusion.part_ref), custom_call_target="tpu_custom_call" | custom-call | tf_op jit(solution)/shard_map/pallas_call | solution.py:108
  60.7 0.6 select_reduce_fusion.2
  (8 shorter events, 0.1 us)
Async XLA Ops:
  0.6 1.2 %copy-start = (bf16[1,1024,512]{2,1,0:T(8,128)(2,1)S(1)}, bf16[1,1024,512]{2,1,0:T(8,128)(2,1)}, u32[]{:S(2)}) copy-start(bf16[1,1024,512]{2,1,0:T(8,128)(2,1)} %param.7) | copy-start | bytes 3145732
  4.9 0.7 %copy-start.1 = (f32[4096]{0:T(1024)S(1)}, f32[4096]{0:T(1024)}, u32[]{:S(2)}) copy-start(f32[4096]{0:T(1024)} %param.8) | copy-start | bytes 49156
  5.6 37.9 %copy-start.2 = (bf16[4096,512]{1,0:T(8,128)(2,1)S(1)}, bf16[4096,512]{1,0:T(8,128)(2,1)}, u32[]{:S(2)}) copy-start(bf16[4096,512]{1,0:T(8,128)(2,1)} %param.9) | copy-start | bytes 12582916

commit v15 on v11

--- a/solution.py
+++ b/solution.py
@@ -63,9 +63,7 @@
     own1.start()
 
     def finish1(i, carry):
-        p = lax.rem(me + 1 + i, n_dp)
-        in1(p).wait_recv()
-        out1(p).wait_send()
+        in1(lax.rem(me + 1 + i, n_dp)).wait_recv()
         return carry
 
     lax.fori_loop(0, n_dp - 1, finish1, 0)
@@ -92,15 +90,24 @@
     own2.start()
 
     def finish2(i, carry):
-        q = lax.rem(mt + 1 + i, n_t)
-        in2(q).wait_recv()
-        out2(q).wait_send()
+        in2(lax.rem(mt + 1 + i, n_t)).wait_recv()
         return carry
 
     lax.fori_loop(0, n_t - 1, finish2, 0)
     own2.wait()
 
     out_ref[...] = merge(got2[...])
+
+    def drain1(i, carry):
+        out1(lax.rem(me + 1 + i, n_dp)).wait_send()
+        return carry
+
+    def drain2(i, carry):
+        out2(lax.rem(mt + 1 + i, n_t)).wait_send()
+        return carry
+
+    lax.fori_loop(0, n_dp - 1, drain1, 0)
+    lax.fori_loop(0, n_t - 1, drain2, 0)
 
 
 def exchange_stats(parts, n_t):

time: 61.6 us -> 61.9 us (level)
  no operation moved by 1% of the time
where the time goes in v15:
time: 61.9 us; the launch traced here: 61.7 us
  Pallas kernels  52.1 us (84%)
  local copies, waits for them, and re-layouts  3.04 us (5%)
  other arithmetic  2.77 us (4%)
  matrix products  2.38 us (4%)
  between operations  1.4 us (2%)
    pallas_call x1, Pallas kernels, gather_rows(): pl.pallas_call(rows_kernel, out_shape=jax.ShapeDtypeStruct((n_dp,) + shap...  38.5 us
    pallas_call x1, Pallas kernels, exchange_stats(): pl.pallas_call(stats_kernel, out_shape=jax.ShapeDtypeStruct((four, k), jn...  13.6 us
    dot_general x1, matrix products, per_device(): logits = jnp.dot(rows_piece, head, preferred_element_type=jnp.float32)  2.38 us
    unnamed x7, local copies, waits for them, and re-layouts  2.05 us

profile of v15, /device:TPU:1, one launch (start us, length us, event | category | flops | bytes accessed | tf_op | source)
XLA Modules:
  0.0 61.7 jit_solution(12265367119492818681)
XLA Ops:
  0.6 0.0 copy-start
  0.6 1.2 %copy-done = bf16[1,1024,512]{2,1,0:T(8,128)(2,1)S(1)} copy-done((bf16[1,1024,512]{2,1,0:T(8,128)(2,1)S(1)}, bf16[1,1024,512]{2,1,0:T(8,128)(2,1)}, u32[]{:S(2)}) %copy-start) | copy-done | bytes 1048600
  1.9 0.7 %compare_bitcast_fusion = (pred[32]{0:T(512)(128)(4,1)S(1)}, s32[32]{0:T(128)S(1)}) fusion(s32[1,32]{1,0:T(1,128)} %param.13), kind=kLoop, calls=%fused_computation.30 | loop fusion | flops 96 | bytes 288 | tf_op jit(solution)/shard_map/and | solution.py:315
  2.5 0.1 select_reduce_fusion.1
  2.6 0.8 %select_reduce_fusion.4 = (s32[16]{0:T(128)S(1)}, s32[16]{0:T(128)S(1)}, s32[16]{0:T(128)S(1)}) fusion(s32[32]{0:T(128)} %bitcast.42, s32[32]{0:T(128)S(1)} %get-tuple-element.19, pred[32]{0:T(512)(128)(4,1)S(1)} %get-tuple-element.14, s32[32]{0:T(128)} %bitcast.43, s32[32]{0:T(128)S(1)} %get-tuple-element.18), kind=kLoop, calls=%fused_computation.14 | loop fusion | flops 4048 | bytes 736 | tf_op jit(solution)/shard_map/reduce_sum | solution.py:318
  4.2 0.6 gather_fusion
  4.8 0.1 broadcast_select_fusion.rows_ref
  4.8 0.1 copy.16.target_ref
  4.9 0.0 copy-start.1
  4.9 0.7 %copy-done.1 = f32[4096]{0:T(1024)S(1)} copy-done((f32[4096]{0:T(1024)S(1)}, f32[4096]{0:T(1024)}, u32[]{:S(2)}) %copy-start.1) | copy-done | bytes 16408
  5.6 0.0 copy-start.2
  5.6 38.5 %shard_map.86 = bf16[32,16,4224]{2,1,0:T(8,128)(2,1)S(1)} custom-call(bf16[16,512]{1,0:T(8,128)(2,1)S(1)} %broadcast_select_fusion.rows_ref, f32[1,4096]{1,0:T(1,128)S(1)} %bitcast.33, s32[16,1]{1,0:T(8,128)S(1)} %copy.16.target_ref), custom_call_target="tpu_custom_call" | custom-call | tf_op jit(solution)/shard_map/pallas_call | solution.py:286
  44.2 0.0 copy-done.2
  44.2 2.4 %fusion.12 = (f32[512]{0:T(512)S(1)}, f32[512,512]{0,1:T(8,128)S(1)}) fusion(bf16[4096,512]{1,0:T(8,128)(2,1)S(1)} %copy-done.2, bf16[512,4224]{1,0:T(8,128)(2,1)S(1)} %bitcast.31), kind=kOutput, calls=%fused_computation.44 | convolution fusion | flops 2147745280 | bytes 9439232 | tf_op jit(solution)/shard_map/dot_general | solution.py:332
  46.6 0.1 copy.22
  46.7 0.3 fusion.2
  47.1 0.1 stack.18
  47.1 0.1 stack.17
  47.2 0.1 stack.16
  47.3 0.1 stack.15
  47.4 0.1 maximum_bitcast_fusion.part_ref
  47.5 13.6 %shard_map.87 = f32[4,16]{1,0:T(4,128)S(1)} custom-call(f32[32,4,16]{2,1,0:T(4,128)S(1)} %maximum_bitcast_fusion.part_ref), custom_call_target="tpu_custom_call" | custom-call | tf_op jit(solution)/shard_map/pallas_call | solution.py:115
  61.1 0.6 select_reduce_fusion.2
  (8 shorter events, 0.1 us)
Async XLA Ops:
  0.6 1.2 %copy-start = (bf16[1,1024,512]{2,1,0:T(8,128)(2,1)S(1)}, bf16[1,1024,512]{2,1,0:T(8,128)(2,1)}, u32[]{:S(2)}) copy-start(bf16[1,1024,512]{2,1,0:T(8,128)(2,1)} %param.7) | copy-start | bytes 3145732
  4.9 0.7 %copy-start.1 = (f32[4096]{0:T(1024)S(1)}, f32[4096]{0:T(1024)}, u32[]{:S(2)}) copy-start(f32[4096]{0:T(1024)} %param.8) | copy-start | bytes 49156
  5.6 38.5 %copy-start.2 = (bf16[4096,512]{1,0:T(8,128)(2,1)S(1)}, bf16[4096,512]{1,0:T(8,128)(2,1)}, u32[]{:S(2)}) copy-start(bf16[4096,512]{1,0:T(8,128)(2,1)} %param.9) | copy-start | bytes 12582916

commit v16 on v11

--- a/solution.py
+++ b/solution.py
@@ -183,9 +183,7 @@
     own_t.start()
 
     def t_finish(i, carry):
-        q = lax.rem(mt + 1 + i, n_t)
-        t_in(q).wait_recv()
-        t_out(q).wait_send()
+        t_in(lax.rem(mt + 1 + i, n_t)).wait_recv()
         return carry
 
     lax.fori_loop(0, n_t - 1, t_finish, 0)
@@ -271,6 +269,12 @@
     for copy in sends:
         copy.wait_send()
     own.wait()
+
+    def t_drain(i, carry):
+        t_out(lax.rem(mt + 1 + i, n_t)).wait_send()
+        return carry
+
+    lax.fori_loop(0, n_t - 1, t_drain, 0)
 
 
 def gather_rows(rows, gain, target, n_dp, n_t):

time: 61.6 us -> 61.6 us (level)
  no operation moved by 1% of the time
where the time goes in v16:
time: 61.6 us; the launch traced here: 61.4 us
  Pallas kernels  51.8 us (84%)
  local copies, waits for them, and re-layouts  3.04 us (5%)
  other arithmetic  2.77 us (4%)
  matrix products  2.39 us (4%)
  between operations  1.4 us (2%)
    pallas_call x1, Pallas kernels, gather_rows(): pl.pallas_call(rows_kernel, out_shape=jax.ShapeDtypeStruct((n_dp,) + shap...  38.6 us
    pallas_call x1, Pallas kernels, exchange_stats(): pl.pallas_call(stats_kernel, out_shape=jax.ShapeDtypeStruct((four, k), jn...  13.3 us
    dot_general x1, matrix products, per_device(): logits = jnp.dot(rows_piece, head, preferred_element_type=jnp.float32)  2.39 us
    unnamed x7, local copies, waits for them, and re-layouts  2.05 us

profile of v16, /device:TPU:1, one launch (start us, length us, event | category | flops | bytes accessed | tf_op | source)
XLA Modules:
  0.0 61.4 jit_solution(3908425350373886373)
XLA Ops:
  0.6 0.0 copy-start
  0.6 1.2 %copy-done = bf16[1,1024,512]{2,1,0:T(8,128)(2,1)S(1)} copy-done((bf16[1,1024,512]{2,1,0:T(8,128)(2,1)S(1)}, bf16[1,1024,512]{2,1,0:T(8,128)(2,1)}, u32[]{:S(2)}) %copy-start) | copy-done | bytes 1048600
  1.9 0.7 %compare_bitcast_fusion = (pred[32]{0:T(512)(128)(4,1)S(1)}, s32[32]{0:T(128)S(1)}) fusion(s32[1,32]{1,0:T(1,128)} %param.13), kind=kLoop, calls=%fused_computation.30 | loop fusion | flops 96 | bytes 288 | tf_op jit(solution)/shard_map/and | solution.py:312
  2.5 0.1 select_reduce_fusion.1
  2.6 0.8 %select_reduce_fusion.4 = (s32[16]{0:T(128)S(1)}, s32[16]{0:T(128)S(1)}, s32[16]{0:T(128)S(1)}) fusion(s32[32]{0:T(128)} %bitcast.42, s32[32]{0:T(128)S(1)} %get-tuple-element.19, pred[32]{0:T(512)(128)(4,1)S(1)} %get-tuple-element.14, s32[32]{0:T(128)} %bitcast.43, s32[32]{0:T(128)S(1)} %get-tuple-element.18), kind=kLoop, calls=%fused_computation.14 | loop fusion | flops 4048 | bytes 736 | tf_op jit(solution)/shard_map/reduce_sum | solution.py:315
  4.2 0.6 gather_fusion
  4.8 0.1 broadcast_select_fusion.rows_ref
  4.8 0.1 copy.16.target_ref
  4.9 0.0 copy-start.1
  4.9 0.7 %copy-done.1 = f32[4096]{0:T(1024)S(1)} copy-done((f32[4096]{0:T(1024)S(1)}, f32[4096]{0:T(1024)}, u32[]{:S(2)}) %copy-start.1) | copy-done | bytes 16408
  5.6 0.0 copy-start.2
  5.6 38.6 %shard_map.86 = bf16[32,16,4224]{2,1,0:T(8,128)(2,1)S(1)} custom-call(bf16[16,512]{1,0:T(8,128)(2,1)S(1)} %broadcast_select_fusion.rows_ref, f32[1,4096]{1,0:T(1,128)S(1)} %bitcast.33, s32[16,1]{1,0:T(8,128)S(1)} %copy.16.target_ref), custom_call_target="tpu_custom_call" | custom-call | tf_op jit(solution)/shard_map/pallas_call | solution.py:283
  44.2 0.0 copy-done.2
  44.2 2.4 %fusion.12 = (f32[512]{0:T(512)S(1)}, f32[512,512]{0,1:T(8,128)S(1)}) fusion(bf16[4096,512]{1,0:T(8,128)(2,1)S(1)} %copy-done.2, bf16[512,4224]{1,0:T(8,128)(2,1)S(1)} %bitcast.31), kind=kOutput, calls=%fused_computation.44 | convolution fusion | flops 2147745280 | bytes 9439232 | tf_op jit(solution)/shard_map/dot_general | solution.py:329
  46.6 0.1 copy.22
  46.8 0.3 fusion.2
  47.1 0.1 stack.18
  47.2 0.1 stack.17
  47.3 0.1 stack.16
  47.4 0.1 stack.15
  47.4 0.1 maximum_bitcast_fusion.part_ref
  47.5 13.3 %shard_map.87 = f32[4,16]{1,0:T(4,128)S(1)} custom-call(f32[32,4,16]{2,1,0:T(4,128)S(1)} %maximum_bitcast_fusion.part_ref), custom_call_target="tpu_custom_call" | custom-call | tf_op jit(solution)/shard_map/pallas_call | solution.py:108
  60.8 0.6 select_reduce_fusion.2
  (8 shorter events, 0.1 us)
Async XLA Ops:
  0.6 1.2 %copy-start = (bf16[1,1024,512]{2,1,0:T(8,128)(2,1)S(1)}, bf16[1,1024,512]{2,1,0:T(8,128)(2,1)}, u32[]{:S(2)}) copy-start(bf16[1,1024,512]{2,1,0:T(8,128)(2,1)} %param.7) | copy-start | bytes 3145732
  4.9 0.7 %copy-start.1 = (f32[4096]{0:T(1024)S(1)}, f32[4096]{0:T(1024)}, u32[]{:S(2)}) copy-start(f32[4096]{0:T(1024)} %param.8) | copy-start | bytes 49156
  5.6 38.6 %copy-start.2 = (bf16[4096,512]{1,0:T(8,128)(2,1)S(1)}, bf16[4096,512]{1,0:T(8,128)(2,1)}, u32[]{:S(2)}) copy-start(bf16[4096,512]{1,0:T(8,128)(2,1)} %param.9) | copy-start | bytes 12582916
